TPU v7x, 32 devices: a whole 2x2x4 slice. The times are simulated.
32 devices in a mesh: tm: 16 (over z, y, x), head: 2 (over core).
Axes of the slice: x: 2, y: 2, z: 4, core: 2. Of those that a mesh axis runs over, the one named last changes fastest.
Arguments:
- patches: bfloat16 [192, 256, 1152], P('tm', None, 'head'), may hold values from -6 to 6
- grid_rows: int32 [192], P('tm'), may hold values from 8 to 16
- frame_ids: int32 [192], P('tm'), may hold values from 0 to 191, as said below
- ln_gain: float32 [1152], replicated, may hold values from 0.1 to 1.9
- w_qkv: bfloat16 [3, 1152, 1152], P(None, None, 'head'), may hold values from -5.9514821 to 5.9514821
- w_out: bfloat16 [1152, 1152], P('head'), may hold values from -0.1875 to 0.1875
- w_conn: bfloat16 [1152, 4096], P(None, 'head'), may hold values from -0.1875 to 0.1875
- norm_gain: float32 [4096], replicated, may hold values from 0.1 to 1.9
- w_x: bfloat16 [4096, 4096], P(None, 'head'), may hold values from -0.09375 to 0.09375
- w_b: bfloat16 [4096, 1024], P(None, 'head'), may hold values from -0.09375 to 0.09375
- w_c: bfloat16 [4096, 1024], P(None, 'head'), may hold values from -0.09375 to 0.09375
- w_dt: bfloat16 [4096, 64], P(None, 'head'), may hold values from -0.09375 to 0.09375
- dt_bias: float32 [64], P('head'), may hold values from -1 to 1
- a_log: float32 [64], P('head'), may hold values from -14 to -3.2
- d_skip: float32 [64], P('head'), may hold values from 0.5 to 1.5
- out_gain: float32 [4096], P('head'), may hold values from 0.1 to 1.9
Outputs:
- stream: bfloat16 [12288, 4096], P('tm', 'head')
- ssd_out: bfloat16 [12288, 4096], P('tm', 'head')
Inputs may be any that keep to these rules, and one draw needn't show every extreme that they name: frame_ids is a permutation of the frames; the 12 slots of one tm index hold frames of 12 different time shards, time shard of a frame being frame // 12.
All inputs are finite; a program needn't handle non-finite values.
Results may differ from a plain program's by a relative error of at most 0.013.
Values may be sent and summed in bfloat16 or wider, within the bound.
A program may use at most 128 MiB of HBM per device.

v0:
```python
import jax
import jax.numpy as jnp
from jax import lax
from jax.sharding import PartitionSpec as P

GRID = 16
POOL = 4
VHD = 72
HDIM = 64
STATE = 128
STRETCH = 256


highest = lax.Precision.HIGHEST


def carried_in(value, axis, combine, identity):
    count, position = (lax.axis_size(axis), lax.axis_index(axis))
    everything = jax.tree.map(
        lambda part, kind: lax.all_gather(part.astype(kind), axis),
        value,
        (jnp.bfloat16, jnp.bfloat16),
    )
    start = jax.tree.map(
        lambda part, zero: jnp.broadcast_to(jnp.asarray(zero, part.dtype), part.shape),
        value,
        identity,
    )

    def step(k, before):
        reached = k < position
        new = combine(
            before, jax.tree.map(lambda part, own: part[k].astype(own.dtype), everything, value)
        )
        return jax.tree.map(lambda a, b: jnp.where(reached, a, b), new, before)

    return lax.fori_loop(0, count, step, start)


def layer_norm(rows, gain):
    values = rows.astype(jnp.float32)
    centre = jnp.mean(values, axis=-1, keepdims=True)
    spread = jnp.mean(jnp.square(values - centre), axis=-1, keepdims=True)
    return ((values - centre) * lax.rsqrt(spread + 1e-06) * gain).astype(jnp.bfloat16)


def attend(full_patches, valid_count, ln_gain, w_qkv, w_out):
    frame_count, patch_count, full_width = full_patches.shape
    local_width = w_qkv.shape[2]
    local_heads = local_width // VHD
    normed = layer_norm(full_patches, ln_gain).reshape(frame_count * patch_count, full_width)
    triple = jnp.einsum("rc,mcd->mrd", normed, w_qkv, preferred_element_type=jnp.float32).astype(
        jnp.bfloat16
    )
    triple = triple.reshape(3, frame_count, patch_count, local_heads, VHD)
    scores = jnp.einsum(
        "fqhd,fkhd->fhqk", triple[0], triple[1], preferred_element_type=jnp.float32
    ) * VHD ** (-0.5)
    usable = jnp.arange(patch_count)[None, :] < valid_count[:, None]
    scores = jnp.where(usable[:, None, None, :], scores, -1e30)
    row_max = jnp.max(scores, axis=-1, keepdims=True)
    powered = jnp.exp(scores - row_max)
    weights_soft = (powered / jnp.sum(powered, axis=-1, keepdims=True)).astype(jnp.bfloat16)
    context = jnp.einsum(
        "fhqk,fkhd->fqhd", weights_soft, triple[2], preferred_element_type=jnp.float32
    ).astype(jnp.bfloat16)
    attended = jnp.dot(
        context.reshape(frame_count * patch_count, local_width),
        w_out,
        preferred_element_type=jnp.float32,
    )
    return jnp.mean(attended.reshape(frame_count, patch_count // POOL, POOL, full_width), axis=2)


def bucket_frames(owned, frame_ids, shards):
    frame_count = owned.shape[0]
    target = frame_ids // frame_count
    onehot = target[None, :] == jnp.arange(shards)[:, None]
    outgoing = jnp.einsum(
        "tf,fpc->tpc", onehot.astype(owned.dtype), owned, preferred_element_type=jnp.float32
    ).astype(owned.dtype)
    labels = jnp.sum(jnp.where(onehot, frame_ids[None, :] + 1, 0), axis=1)
    return (outgoing, labels)


def place_frames(incoming, arrived, frame_count):
    first_frame = lax.axis_index("tm") * frame_count
    local_frame = arrived - 1 - first_frame
    onehot = jnp.arange(frame_count)[:, None] == local_frame[None, :]
    placed = jnp.einsum(
        "ft,tpc->fpc", onehot.astype(incoming.dtype), incoming, preferred_element_type=jnp.float32
    ).astype(incoming.dtype)
    return placed.reshape(frame_count * incoming.shape[1], incoming.shape[2])


def project(stream_rows, norm_gain, w_x, w_b, w_c, w_dt, dt_bias, a_log):
    values = stream_rows.astype(jnp.float32)
    normed = (
        values * lax.rsqrt(jnp.mean(values * values, axis=-1, keepdims=True) + 1e-05) * norm_gain
    ).astype(jnp.bfloat16)
    inner_rows = jnp.dot(normed, w_x, preferred_element_type=jnp.float32).astype(jnp.bfloat16)
    write_keys = jnp.dot(normed, w_b, preferred_element_type=jnp.float32).astype(jnp.bfloat16)
    read_keys = jnp.dot(normed, w_c, preferred_element_type=jnp.float32).astype(jnp.bfloat16)
    step_size = jax.nn.softplus(jnp.dot(normed, w_dt, preferred_element_type=jnp.float32) + dt_bias)
    log_decay = -jnp.exp(a_log) * step_size
    return (inner_rows, write_keys, read_keys, step_size, log_decay)


def ssd_stretch(inner_rows, write_keys, read_keys, step_size, log_decay, d_skip, state):
    length = inner_rows.shape[0]
    head_count = step_size.shape[1]
    groups = write_keys.shape[1] // STATE
    per_group = head_count // groups
    cumul = jnp.cumsum(log_decay, axis=0)
    scaled = (
        inner_rows.astype(jnp.float32).reshape(length, head_count, HDIM) * step_size[:, :, None]
    )
    writers = write_keys.astype(jnp.float32).reshape(length, groups, STATE)
    readers = read_keys.astype(jnp.float32).reshape(length, groups, STATE)
    intersection = jnp.einsum("tgn,sgn->gts", readers, writers, precision=highest)
    causal = (jnp.arange(length)[:, None] >= jnp.arange(length)[None, :])[:, :, None]
    spans = cumul[:, None, :] - cumul[None, :, :]
    decays = jnp.where(causal, jnp.exp(jnp.where(causal, spans, 0.0)), 0.0)
    mixing = jnp.repeat(intersection, per_group, axis=0) * jnp.transpose(decays, (2, 0, 1))
    within = jnp.einsum("hts,shp->thp", mixing, scaled, precision=highest)
    carried = (
        jnp.einsum(
            "tgn,gkpn->tgkp",
            readers,
            state.reshape(groups, per_group, HDIM, STATE),
            precision=highest,
        ).reshape(length, head_count, HDIM)
        * jnp.exp(cumul)[:, :, None]
    )
    remaining = jnp.exp(cumul[-1][None, :] - cumul)
    fresh_state = jnp.einsum(
        "sgkp,sgn->gkpn",
        (scaled * remaining[:, :, None]).reshape(length, groups, per_group, HDIM),
        writers,
        precision=highest,
    ).reshape(head_count, HDIM, STATE)
    new_state = jnp.exp(cumul[-1])[:, None, None] * state + fresh_state
    outputs = (
        within
        + carried
        + d_skip[None, :, None] * inner_rows.astype(jnp.float32).reshape(length, head_count, HDIM)
    )
    return (outputs, new_state, cumul)


def group_norm(outputs, out_gain, groups):
    length = outputs.shape[0]
    grouped = outputs.reshape(length, groups, -1)
    normed = grouped * lax.rsqrt(jnp.mean(grouped * grouped, axis=-1, keepdims=True) + 1e-05)
    return (normed.reshape(length, -1) * out_gain).astype(jnp.bfloat16)


def combine_states(earlier, later):
    return (earlier[0] + later[0], jnp.exp(later[0])[:, None, None] * earlier[1] + later[1])


def on_device(
    patches,
    grid_rows,
    frame_ids,
    ln_gain,
    w_qkv,
    w_out,
    w_conn,
    norm_gain,
    w_x,
    w_b,
    w_c,
    w_dt,
    dt_bias,
    a_log,
    d_skip,
    out_gain,
):
    frame_count, patch_count, slice_width = patches.shape
    tokens_frame = patch_count // POOL
    shards = lax.axis_size("tm")
    full_patches = lax.all_gather(patches, "head", axis=2, tiled=True)
    full_width = full_patches.shape[2]
    valid_count = grid_rows * GRID
    attn_pooled = attend(full_patches, valid_count, ln_gain, w_qkv, w_out)
    kept_tokens = (jnp.arange(tokens_frame)[None, :] * POOL < valid_count[:, None])[:, :, None]
    summed_attn = lax.psum(attn_pooled, "head")
    pooled_patches = jnp.mean(
        full_patches.astype(jnp.float32).reshape(frame_count, tokens_frame, POOL, full_width),
        axis=2,
    )
    vision = jnp.where(kept_tokens, pooled_patches + summed_attn, 0.0).astype(jnp.bfloat16)
    projected = jnp.dot(
        vision.reshape(frame_count * tokens_frame, full_width),
        w_conn,
        preferred_element_type=jnp.float32,
    ).astype(jnp.bfloat16)
    outgoing, labels = bucket_frames(
        projected.reshape(frame_count, tokens_frame, w_conn.shape[1]), frame_ids, shards
    )
    incoming, arrived = (
        lax.all_to_all(outgoing, "tm", split_axis=0, concat_axis=0, tiled=True),
        lax.all_to_all(labels, "tm", split_axis=0, concat_axis=0, tiled=True),
    )
    stream_rows = place_frames(incoming, arrived, frame_count)
    wide = lax.all_gather(stream_rows, "head", axis=1, tiled=True)
    token_count = wide.shape[0]
    local_heads = w_dt.shape[1]
    groups = w_b.shape[1] // STATE
    per_group = local_heads // groups
    projected_rows = project(wide, norm_gain, w_x, w_b, w_c, w_dt, dt_bias, a_log)
    stretch_count = token_count // STRETCH
    sliced = tuple(
        (member.reshape(stretch_count, STRETCH, member.shape[1]) for member in projected_rows)
    )

    def stretch_step(state, pieces):
        outputs, new_state, cumul = ssd_stretch(
            pieces[0], pieces[1], pieces[2], pieces[3], pieces[4], d_skip, state
        )
        return (new_state, (outputs, cumul))

    zero_state = jnp.zeros((local_heads, HDIM, STATE), jnp.float32)
    device_state, (outputs, cumul) = lax.scan(stretch_step, zero_state, sliced)
    totals = cumul[:, -1, :]
    total_log = jnp.sum(totals, axis=0)
    identity = (jnp.zeros_like(total_log), jnp.zeros_like(device_state))
    incoming_state = carried_in((total_log, device_state), "tm", combine_states, identity)[1]
    offsets = jnp.cumsum(totals, axis=0) - totals
    from_start = (cumul + offsets[:, None, :]).reshape(token_count, local_heads)
    readers = projected_rows[2].astype(jnp.float32).reshape(token_count, groups, STATE)
    correction = (
        jnp.einsum(
            "tgn,gkpn->tgkp",
            readers,
            incoming_state.reshape(groups, per_group, HDIM, STATE),
            precision=highest,
        ).reshape(token_count, local_heads, HDIM)
        * jnp.exp(from_start)[:, :, None]
    )
    combined = outputs.reshape(token_count, local_heads, HDIM) + correction
    return (stream_rows, group_norm(combined, out_gain, groups))


def solution(mesh):
    in_specs = (
        P("tm", None, "head"),
        P("tm"),
        P("tm"),
        P(),
        P(None, None, "head"),
        P("head", None),
        P(None, "head"),
        P(),
        P(None, "head"),
        P(None, "head"),
        P(None, "head"),
        P(None, "head"),
        P("head"),
        P("head"),
        P("head"),
        P("head"),
    )
    out_specs = (P("tm", "head"), P("tm", "head"))
    return jax.shard_map(
        on_device, mesh=mesh, in_specs=in_specs, out_specs=out_specs, check_vma=False
    )
```

profile of v0, /device:TPU:0, one launch (start us, length us, event | category | flops | bytes accessed | tf_op | source)
XLA Modules:
  0.0 784.3 jit_solution(12642048657780200994)
XLA Ops:
  8.7 21.5 %all-gather.6.cloned.1.call-done = bf16[12,256,1152]{1,2,0:T(8,128)(2,1)} async-done(((bf16[12,256,576]{1,2,0:T(8,128)(2,1)}), bf16[12,256,1152]{1,2,0:T(8,128)(2,1)}) %all-gather.6.cloned.1.call-update) | async-done | bytes 7077904 | tf_op jit(solution)/shard_map/all_gather | solution.py:183
  30.2 10.3 %copy.121 = bf16[12,256,1152]{2,1,0:T(8,128)(2,1)} copy(bf16[12,256,1152]{1,2,0:T(8,128)(2,1)} %all-gather.6.cloned.1.call-done) | data formatting | bytes 14155776 | tf_op jit(solution)/shard_map/all_gather | solution.py:183
  40.5 4.2 convert_reduce_fusion
  45.6 2.0 multiply_reduce_fusion
  47.6 2.4 multiply_convert_fusion
  50.0 15.7 %convert_bitcast_fusion = bf16[3,3072,576]{1,2,0:T(8,128)(2,1)S(1)} fusion(bf16[3072,1152,1]{1,0,2:T(8,128)(2,1)S(1)} %bitcast.239, bf16[3,1152,576]{1,2,0:T(8,128)(2,1)} %param.24), kind=kOutput, calls=%fused_computation.52 | convolution fusion | flops 12235898880 | bytes 21676032 | tf_op jit(solution)/shard_map/rc,mcd->mrd/dot_general | solution.py:52
  65.7 4.1 fusion.96
  69.9 7.2 squeeze.32
  77.1 7.3 squeeze.33
  84.5 7.2 squeeze.31
  91.7 16.0 %fusion.97 = f32[12,8,256]{2,1,0:T(8,128)S(1)} fusion(pred[12,256]{1,0:T(8,128)(4,1)S(1)} %iota_compare_fusion.1, bf16[12,256,8,72]{1,0,3,2:T(8,128)(2,1)} %squeeze.33, bf16[12,256,8,72]{1,0,3,2:T(8,128)(2,1)} %squeeze.32), kind=kOutput, calls=%fused_computation.120 | convolution fusion | flops 931135744 | bytes 7179264 | tf_op jit(solution)/shard_map/sub | solution.py:62
  107.7 21.8 %convert_bitcast_fusion.1 = bf16[12,256,8,72]{1,3,2,0:T(8,128)(2,1)} fusion(f32[12,8,256]{2,1,0:T(8,128)S(1)} %fusion.97, pred[12,256]{1,0:T(8,128)(4,1)S(1)} %iota_compare_fusion.1, bf16[12,256,8,72]{1,0,3,2:T(8,128)(2,1)} %squeeze.31, bf16[12,256,8,72]{1,0,3,2:T(8,128)(2,1)} %squeeze.33, bf16[12,256,8,72]{1,0,3,2:T(8,128)(2,1)} %squeeze.32), kind=kOutput, calls=%fused_computation.71 | convolution fusion | flops 1845190912 | bytes 14257152 | tf_op jit(solution)/shard_map/fhqk,fkhd->fqhd/dot_general | solution.py:64
  129.5 8.0 %copy.126 = bf16[12,256,8,72]{3,2,1,0:T(8,128)(2,1)} copy(bf16[12,256,8,72]{1,3,2,0:T(8,128)(2,1)} %convert_bitcast_fusion.1) | data formatting | bytes 7077888 | tf_op jit(solution)/shard_map/convert_element_type | solution.py:66
  137.6 11.6 %dot_general.53 = bf16[12,64,4,576]{3,2,1,0:T(4,128)(2,1)} reshape(bf16[12,256,8,72]{3,2,1,0:T(8,128)(2,1)} %copy.126) | data formatting | bytes 7077888 | tf_op jit(solution)/shard_map/dot_general | solution.py:67
  149.2 8.4 %fusion.49 = f32[12,64,1152]{2,1,0:T(8,128)S(1)} fusion(bf16[12,64,4,576]{3,2,1,0:T(4,128)(2,1)} %dot_general.53, bf16[576,1152]{1,0:T(8,128)(2,1)S(1)} %copy-done), kind=kOutput, calls=%fused_computation.74 | convolution fusion | flops 4079517696 | bytes 8404992 | tf_op jit(solution)/shard_map/dot_general | solution.py:67
  157.7 2.2 broadcast_multiply_fusion
  160.7 6.8 all-to-all-start
  167.6 14.0 %reshape.268 = f32[12,64,4,1152]{3,2,1,0:T(4,128)} reshape(bf16[12,256,1152]{2,1,0:T(8,128)(2,1)} %copy.121) | data formatting | bytes 21233664 | tf_op jit(solution)/shard_map/reshape | solution.py:190
  181.6 13.0 %reduce_sum.89 = f32[12,64,1152]{2,1,0:T(8,128)} reduce(f32[12,64,4,1152]{3,2,1,0:T(4,128)} %reshape.268, f32[]{:T(128)} %constant.94.clone.1), dimensions={2}, to_apply=%region_1.0 | reduce | flops 2654208 | bytes 17694724 | tf_op jit(solution)/shard_map/reduce_sum | solution.py:189
  194.5 3.5 select_convert_fusion
  198.1 6.9 convolution_convert_fusion.1
  205.0 2.3 fusion.38
  207.3 4.3 copy.129
  211.6 7.0 all-to-all-start.1
  219.0 79.3 %all-to-all-done.1 = bf16[16,64,2048]{2,1,0:T(8,128)(2,1)} async-done(((bf16[16,64,2048]{2,1,0:T(8,128)(2,1)}), bf16[16,64,2048]{2,1,0:T(8,128)(2,1)}, u32[]{:S(2)}, u32[]{:S(2)}) %all-to-all-start.1) | async-done | bytes 4194336 | tf_op jit(solution)/shard_map/all_to_all | solution.py:203
  298.3 7.0 fusion.41
  305.3 3.4 copy.131
  309.0 31.1 %all-gather.8.cloned.1.call-done = bf16[768,4096]{1,0:T(8,128)(2,1)} async-done(((bf16[768,2048]{1,0:T(8,128)(2,1)}), bf16[768,4096]{1,0:T(8,128)(2,1)}) %all-gather.8.cloned.1.call-update) | async-done | bytes 6291472 | tf_op jit(solution)/shard_map/all_gather | solution.py:207
  340.1 4.2 fusion.19
  344.7 2.1 broadcast_multiply_fusion.1
  347.0 8.5 %convolution_convert_fusion.2 = bf16[768,512]{1,0:T(8,128)(2,1)} fusion(bf16[4096,512]{1,0:T(8,128)(2,1)} %param.30, bf16[768,4096]{1,0:T(8,128)(2,1)} %all-gather.8.cloned.1.call-done, f32[4096]{0:T(1024)S(1)} %copy-done.13, f32[768]{0:T(1024)S(1)} %add_rsqrt_fusion.2), kind=kOutput, calls=%fused_computation.83 | convolution fusion | flops 3234201600 | bytes 11291648 | tf_op jit(solution)/shard_map/dot_general | solution.py:103
  355.5 4.4 convolution_convert_fusion.3
  359.9 17.9 %convolution_convert_fusion = bf16[768,2048]{1,0:T(8,128)(2,1)} fusion(bf16[4096,2048]{1,0:T(8,128)(2,1)} %param.28, bf16[768,4096]{1,0:T(8,128)(2,1)S(1)} %bitcast.241, f32[4096]{0:T(1024)S(1)} %copy-done.13, f32[768]{0:T(1024)S(1)} %add_rsqrt_fusion.2), kind=kOutput, calls=%fused_computation.72 | convolution fusion | flops 12899057664 | bytes 26233856 | tf_op jit(solution)/shard_map/dot_general | solution.py:101
  377.8 225.1 %while.29 = (s32[]{:T(128)}, f32[32,64,128]{2,1,0:T(8,128)}, f32[3,256,32,64]{1,0,3,2:T(4,128)}, f32[3,256,32]{1,2,0:T(8,128)}, f32[3,256,32]{1,0,2:T(4,128)S(1)...) while((s32[]{:T(128)}, f32[32,64,128]{2,1,0:T(8,128)}, ...), condition=%wide.region_12.13_spmd.clone, body=%wide.region_9.12_spmd.clone.sunk | while | flops 3302842368 | bytes 56987660 | solution.py:225
  384.0 2.9 fusion.146
  387.0 2.4 bitcast_add_fusion.2
  391.2 1.9 fusion.147
  394.4 1.9 bitcast_multiply_fusion.4
  396.4 8.0 %fusion.149 = f32[1,256,32,64]{1,3,2,0:T(8,128)S(1)} fusion(f32[256,32,64]{0,2,1:T(8,128)S(1)} %bitcast.224, f32[4,256,8,64]{1,3,2,0:T(8,128)S(1)} %fusion.147, f32[32,256,256]{2,1,0:T(8,128)S(1)} %bitcast_multiply_fusion.4, f32[32]{0:T(128)S(1)} %get-tuple-element.461, f32[256,32]{0,1:T(8,128)S(1)} %get-tuple-element.420, f32[256,32]{0,1:T(8,128)S(1)} %bitcast.238), kind=kOutput, calls=%fused_computation.12.clone.1 | convolution fusion | flops 1613234176 | bytes 14745728 | tf_op jit(solution)/shard_map/while/body/eval_jaxpr/hts,shp->thp/dot_general | solution.py:125
  404.4 2.2 copy.261
  406.6 45.6 %dynamic_update_slice.14 = f32[3,256,32,64]{1,0,3,2:T(4,128)} dynamic-update-slice(f32[3,256,32,64]{1,0,3,2:T(4,128)} %get-tuple-element.441, f32[1,256,32,64]{1,0,3,2:T(1,128)S(1)} %copy.261, s32[]{:T(128)} %get-tuple-element.439, s32[]{:T(128)} %constant.88.clone.1..sunk, s32[]{:T(128)} %constant.88.clone.1..sunk, s32[]{:T(128)} %constant.88.clone.1..sunk) | dynamic-update-slice | bytes 4194308 | tf_op jit(solution)/shard_map/while/body/jit(dynamic_update_index_in_dim)/dynamic_update_slice | solution.py:225
  458.7 2.9 fusion.146
  461.6 2.7 bitcast_add_fusion.2
  466.1 1.9 fusion.147
  469.4 1.9 bitcast_multiply_fusion.4
  471.3 8.0 %fusion.149 = f32[1,256,32,64]{1,3,2,0:T(8,128)S(1)} fusion(f32[256,32,64]{0,2,1:T(8,128)S(1)} %bitcast.224, f32[4,256,8,64]{1,3,2,0:T(8,128)S(1)} %fusion.147, f32[32,256,256]{2,1,0:T(8,128)S(1)} %bitcast_multiply_fusion.4, f32[32]{0:T(128)S(1)} %get-tuple-element.461, f32[256,32]{0,1:T(8,128)S(1)} %get-tuple-element.420, f32[256,32]{0,1:T(8,128)S(1)} %bitcast.238), kind=kOutput, calls=%fused_computation.12.clone.1 | convolution fusion | flops 1613234176 | bytes 14745728 | tf_op jit(solution)/shard_map/while/body/eval_jaxpr/hts,shp->thp/dot_general | solution.py:125
  479.4 2.2 copy.261
  481.5 45.6 %dynamic_update_slice.14 = f32[3,256,32,64]{1,0,3,2:T(4,128)} dynamic-update-slice(f32[3,256,32,64]{1,0,3,2:T(4,128)} %get-tuple-element.441, f32[1,256,32,64]{1,0,3,2:T(1,128)S(1)} %copy.261, s32[]{:T(128)} %get-tuple-element.439, s32[]{:T(128)} %constant.88.clone.1..sunk, s32[]{:T(128)} %constant.88.clone.1..sunk, s32[]{:T(128)} %constant.88.clone.1..sunk) | dynamic-update-slice | bytes 4194308 | tf_op jit(solution)/shard_map/while/body/jit(dynamic_update_index_in_dim)/dynamic_update_slice | solution.py:225
  533.6 2.9 fusion.146
  536.6 2.7 bitcast_add_fusion.2
  544.3 1.9 bitcast_multiply_fusion.4
  546.3 8.0 %fusion.149 = f32[1,256,32,64]{1,3,2,0:T(8,128)S(1)} fusion(f32[256,32,64]{0,2,1:T(8,128)S(1)} %bitcast.224, f32[4,256,8,64]{1,3,2,0:T(8,128)S(1)} %fusion.147, f32[32,256,256]{2,1,0:T(8,128)S(1)} %bitcast_multiply_fusion.4, f32[32]{0:T(128)S(1)} %get-tuple-element.461, f32[256,32]{0,1:T(8,128)S(1)} %get-tuple-element.420, f32[256,32]{0,1:T(8,128)S(1)} %bitcast.238), kind=kOutput, calls=%fused_computation.12.clone.1 | convolution fusion | flops 1613234176 | bytes 14745728 | tf_op jit(solution)/shard_map/while/body/eval_jaxpr/hts,shp->thp/dot_general | solution.py:125
  554.3 2.2 copy.261
  556.5 45.6 %dynamic_update_slice.14 = f32[3,256,32,64]{1,0,3,2:T(4,128)} dynamic-update-slice(f32[3,256,32,64]{1,0,3,2:T(4,128)} %get-tuple-element.441, f32[1,256,32,64]{1,0,3,2:T(1,128)S(1)} %copy.261, s32[]{:T(128)} %get-tuple-element.439, s32[]{:T(128)} %constant.88.clone.1..sunk, s32[]{:T(128)} %constant.88.clone.1..sunk, s32[]{:T(128)} %constant.88.clone.1..sunk) | dynamic-update-slice | bytes 4194308 | tf_op jit(solution)/shard_map/while/body/jit(dynamic_update_index_in_dim)/dynamic_update_slice | solution.py:225
  603.0 2.1 convert_element_type.127
  613.3 42.8 %all-reduce = bf16[512]{0:T(512)(128)(2,1)S(1)} all-reduce(bf16[512]{0:T(512)(128)(2,1)S(1)} %dynamic-update-slice), channel_id=2, replica_groups=mesh['tm'=16,'head'=2] {'tm'}, use_global_device_ids=true, to_apply=%add | all-reduce | flops 512 | bytes 2048
  656.2 7.6 copy.176
  663.8 55.4 %all-gather.10.cloned.1.call-done = bf16[512,64,128]{2,1,0:T(8,128)(2,1)} async-done(((bf16[32,64,128]{2,1,0:T(8,128)(2,1)}), bf16[512,64,128]{2,1,0:T(8,128)(2,1)}) %all-gather.10.cloned.1.call-update) | async-done | bytes 8388624 | tf_op jit(solution)/shard_map/all_gather | solution.py:20
  719.2 21.4 %while.30 = (s32[]{:T(128)}, f32[32,64,128]{2,1,0:T(8,128)S(1)}, s32[]{:T(128)}, bf16[16,32]{1,0:T(8,128)(2,1)S(1)}, bf16[16,32,64,128]{3,2,1,0:T(8,128)(2,1)}, /*index=5*/s32[]{:T(128)}, s32[]{:T(128)}) while((s32[]{:T(128)}, f32[32,64,128]{2,1,0:T(8,128)S(1)}, s32[]{:T(128)}, bf16[16,32]{1,0:T(8,128)(2,1)S(1)}, ...), condition=%wide.region_15.16_spmd.clone, body=%wide.region_14.15_spmd.clone.sunk | while | flops 1310756 | bytes 2621865 | solution.py:37
  740.6 4.5 fusion.76
  745.1 10.7 %reshape.282 = f32[3,256,32,64]{1,0,3,2:T(4,128)} reshape(f32[768,4,8,64]{0,3,2,1:T(8,128)} %bitcast.226) | data formatting | bytes 12582912 | tf_op jit(solution)/shard_map/reshape | solution.py:239
  755.8 10.0 %multiply_reduce_fusion.1 = f32[3,256,32]{1,0,2:T(4,128)S(1)} fusion(f32[3,256,32,64]{1,0,3,2:T(4,128)} %get-tuple-element.150, f32[3,256,32,64]{1,0,3,2:T(4,128)} %reshape.282, f32[3,256,32]{1,0,2:T(4,128)S(1)} %copy.139), kind=kLoop, calls=%fused_computation.54 | loop fusion | flops 6266880 | bytes 12779520 | tf_op jit(solution)/shard_map/reduce_sum | solution.py:154
  766.0 7.0 fusion.29
  773.0 4.6 copy.142
  (190 shorter events, 63.6 us)
Async XLA Ops:
  7.2 142.0 %copy-start = (bf16[576,1152]{1,0:T(8,128)(2,1)S(1)}, bf16[576,1152]{1,0:T(8,128)(2,1)}, u32[]{:S(2)}) copy-start(bf16[576,1152]{1,0:T(8,128)(2,1)} %param.25) | copy-start | bytes 3981316
  7.2 23.0 %all-gather.6.cloned.1.call-start = ((), (), s32[]{:S(2)}) async-start(), calls=%async_computation.2 | async-start | bytes 10616832 | tf_op jit(solution)/shard_map/all_gather | solution.py:183
  7.9 186.6 %all-reduce.3.cloned.1.call-start = ((), (), s32[]{:S(2)}) async-start(), calls=%async_computation.3 | async-start | bytes 7077888 | tf_op jit(solution)/shard_map/psum | solution.py:188
  40.5 5.0 copy-start.2
  40.5 7.1 copy-start.10
  157.6 2.3 copy-start.14
  160.7 50.9 %all-to-all-start = ((s32[16,1,1]{2,1,0:T(1,128)}), s32[16,1,1]{2,1,0:T(1,128)S(1)}, u32[]{:S(2)}, u32[]{:S(2)}) async-start(s32[16,1,1]{2,1,0:T(1,128)} %copy.120), calls=%async_computation | async-start | bytes 16384 | tf_op jit(solution)/shard_map/all_to_all | solution.py:204
  211.6 86.7 %all-to-all-start.1 = ((bf16[16,64,2048]{2,1,0:T(8,128)(2,1)}), bf16[16,64,2048]{2,1,0:T(8,128)(2,1)}, u32[]{:S(2)}, u32[]{:S(2)}) async-start(bf16[16,64,2048]{2,1,0:T(8,128)(2,1)} %copy.129), calls=%async_computation.1 | async-start | bytes 8388608 | tf_op jit(solution)/shard_map/all_to_all | solution.py:203
  218.6 121.5 %all-gather.8.cloned.1.call-start = ((), (), s32[]{:S(2)}) async-start(), calls=%async_computation.4 | async-start | bytes 9437184 | tf_op jit(solution)/shard_map/all_gather | solution.py:207
  305.3 3.7 copy-start.15
  308.7 35.7 %copy-start.12 = (bf16[4096,32]{0,1:T(8,128)(2,1)S(1)}, bf16[4096,32]{0,1:T(8,128)(2,1)}, u32[]{:S(2)}) copy-start(bf16[4096,32]{0,1:T(8,128)(2,1)} %param.31) | copy-start | bytes 786436
  308.7 35.7 %copy-start.13 = (f32[4096]{0:T(1024)S(1)}, f32[4096]{0:T(1024)}, u32[]{:S(2)}) copy-start(f32[4096]{0:T(1024)} %param.27) | copy-start | bytes 49156
  308.7 35.7 %copy-start.16 = (f32[32]{0:T(128)S(1)}, f32[32]{0:T(128)}, u32[]{:S(2)}) copy-start(f32[32]{0:T(128)} %param.32) | copy-start | bytes 388
  308.7 410.5 %all-gather.10.cloned.1.call-start = ((), (), s32[]{:S(2)}) async-start(), calls=%async_computation.5 | async-start | bytes 8912896 | tf_op jit(solution)/shard_map/all_gather | solution.py:20
  340.1 4.6 copy-start.3
  344.7 10.8 %slice-start = ((s8[6291456]{0:T(1024)(128)(4,1)}), s8[2097152]{0:T(1024)(128)(4,1)S(1)}, s32[]{:S(2)}) async-start(s8[6291456]{0:T(1024)(128)(4,1)} %bitcast.240), calls=%async_computation.6 | async-start | bytes 4194304
  347.0 8.5 %slice-start.1 = ((s8[6291456]{0:T(1024)(128)(4,1)}), s8[4194304]{0:T(1024)(128)(4,1)S(1)}, s32[]{:S(2)}) async-start(s8[6291456]{0:T(1024)(128)(4,1)} %bitcast.240), calls=%async_computation.7 | async-start | bytes 8388608
  347.0 8.5 %copy-start.11 = (bf16[4096,512]{1,0:T(8,128)(2,1)S(1)}, bf16[4096,512]{1,0:T(8,128)(2,1)}, u32[]{:S(2)}) copy-start(bf16[4096,512]{1,0:T(8,128)(2,1)} %param.29) | copy-start | bytes 12582916
  359.9 17.9 %copy-start.8 = (f32[32]{0:T(128)S(1)}, f32[32]{0:T(128)}, u32[]{:S(2)}) copy-start(f32[32]{0:T(128)} %param.34) | copy-start | bytes 388
  378.2 1.9 copy-start.6
  378.2 3.6 copy-start.4
  404.4 48.5 %copy-start.5 = (f32[3,256,32]{1,0,2:T(4,128)S(1)}, f32[3,256,32]{1,0,2:T(4,128)}, u32[]{:S(2)}) copy-start(f32[3,256,32]{1,0,2:T(4,128)} %copy-done.4) | copy-start | bytes 294916 | tf_op jit(solution)/shard_map/while
  404.4 48.5 %copy-start.7 = (f32[3,256,32]{1,0,2:T(4,128)S(1)}, f32[3,256,32]{1,0,2:T(4,128)}, u32[]{:S(2)}) copy-start(f32[3,256,32]{1,0,2:T(4,128)} %copy-done.6) | copy-start | bytes 294916 | tf_op jit(solution)/shard_map/while
  452.9 1.9 copy-start.6
  452.9 3.6 copy-start.4
  479.3 48.5 %copy-start.5 = (f32[3,256,32]{1,0,2:T(4,128)S(1)}, f32[3,256,32]{1,0,2:T(4,128)}, u32[]{:S(2)}) copy-start(f32[3,256,32]{1,0,2:T(4,128)} %copy-done.4) | copy-start | bytes 294916 | tf_op jit(solution)/shard_map/while
  479.3 48.5 %copy-start.7 = (f32[3,256,32]{1,0,2:T(4,128)S(1)}, f32[3,256,32]{1,0,2:T(4,128)}, u32[]{:S(2)}) copy-start(f32[3,256,32]{1,0,2:T(4,128)} %copy-done.6) | copy-start | bytes 294916 | tf_op jit(solution)/shard_map/while
  527.8 1.9 copy-start.6
  527.9 3.6 copy-start.4
  554.3 48.5 %copy-start.5 = (f32[3,256,32]{1,0,2:T(4,128)S(1)}, f32[3,256,32]{1,0,2:T(4,128)}, u32[]{:S(2)}) copy-start(f32[3,256,32]{1,0,2:T(4,128)} %copy-done.4) | copy-start | bytes 294916 | tf_op jit(solution)/shard_map/while
  554.3 48.5 %copy-start.7 = (f32[3,256,32]{1,0,2:T(4,128)S(1)}, f32[3,256,32]{1,0,2:T(4,128)}, u32[]{:S(2)}) copy-start(f32[3,256,32]{1,0,2:T(4,128)} %copy-done.6) | copy-start | bytes 294916 | tf_op jit(solution)/shard_map/while
  755.8 10.1 %copy-start.9 = (f32[2048]{0:T(1024)S(1)}, f32[2048]{0:T(1024)}, u32[]{:S(2)}) copy-start(f32[2048]{0:T(1024)} %param.35) | copy-start | bytes 24580
  766.0 11.6 %copy-start.1 = (bf16[576,1152]{1,0:T(8,128)(2,1)S(1)}, bf16[576,1152]{1,0:T(8,128)(2,1)}, u32[]{:S(2)}) copy-start(bf16[576,1152]{1,0:T(8,128)(2,1)} %param.25) | copy-start | bytes 3981316
Sparse Core Ops, SparseCore 0:
  9.5 20.6 all-gather.5
  160.0 25.2 all-reduce.2
  308.8 31.2 all-gather.7
  605.2 113.9 all-gather.9
where the time goes:
time: 799 us; the launch traced here: 784 us
  local copies, waits for them, and re-layouts  267 us (33%)
  waiting for transfers between devices  188 us (24%)
  matrix products  158 us (20%)
  other arithmetic  97.4 us (12%)
  blocking collectives  42.8 us (5%)
  between operations  15 us (2%)
  starting transfers between devices  14.1 us (2%)
    dynamic_update_slice x6, local copies, waits for them, and re-layouts, on_device(): device_state, (outputs, cumul) = lax.scan(stretch_step, zero_state, sliced)  143 us
    all_to_all x1, waiting for transfers between devices, on_device(): lax.all_to_all(outgoing, 'tm', split_axis=0, concat_axis=0, tiled=True)  79.3 us
    all_gather x1, waiting for transfers between devices, carried_in(): lax.all_gather(part.astype(kind), axis)  55.4 us
    unnamed x1, blocking collectives  42.8 us
    all_gather x1, waiting for transfers between devices, on_device(): wide = lax.all_gather(stream_rows, 'head', axis=1, tiled=True)  31.1 us
    dot_general x3, matrix products, ssd_stretch(): within = jnp.einsum('hts,shp->thp', mixing, scaled, precision=highest)  24 us
    dot_general x1, matrix products, attend(): jnp.einsum('fhqk,fkhd->fqhd', weights_soft, triple[2], preferred_element_...  21.8 us
    all_gather x1, waiting for transfers between devices, on_device(): full_patches = lax.all_gather(patches, 'head', axis=2, tiled=True)  21.5 us
  transfers between devices with their start and end apart: 6, of which 4 were waited for; matrix products, arithmetic and copies ran while one was open for 8% of the time, Pallas kernels for 0%

commit v1 on v0

v1 whole, which is shorter than its diff:
```python
import functools
import math

import jax
import jax.numpy as jnp
from jax import lax
from jax.experimental import pallas as pl
from jax.experimental.pallas import tpu as pltpu
from jax.sharding import PartitionSpec as P

GRID = 16
POOL = 4
VHD = 72
HDIM = 64
STATE = 128
CHUNK = 128
LANES = 128

f32 = jnp.float32
bf16 = jnp.bfloat16
VMEM = pltpu.VMEM
CONTRACT_LAST = (((1,), (1,)), ((), ()))
CONTRACT_FIRST = (((0,), (0,)), ((), ()))


def attend_kernel(
    valid_ref, my_ref, full_ref, own_ref, gain_ref, wqkv_ref, wout_ref, out_ref, normed, context
):
    parts, _, patch_count, part_width = full_ref.shape
    full_width = parts * part_width
    local_width = wqkv_ref.shape[2]
    tokens = patch_count // POOL
    frame = pl.program_id(0)
    pieces = [full_ref[part, 0].astype(f32) for part in range(parts)]
    centre = sum(jnp.sum(piece, axis=-1, keepdims=True) for piece in pieces) / full_width
    pieces = [piece - centre for piece in pieces]
    spread = sum(jnp.sum(piece * piece, axis=-1, keepdims=True) for piece in pieces) / full_width
    scale = lax.rsqrt(spread + 1e-06)
    for part in range(parts):
        normed[:, part * part_width : (part + 1) * part_width] = (
            pieces[part] * scale * gain_ref[part]
        ).astype(bf16)
    rows = normed[...]
    queries, keys, values = [
        jnp.dot(rows, wqkv_ref[member], preferred_element_type=f32).astype(bf16)
        for member in range(3)
    ]
    key_spot = lax.broadcasted_iota(jnp.int32, (1, patch_count), 1)
    bias = jnp.where(key_spot < valid_ref[frame], 0.0, -1e30).astype(f32)
    factor = VHD ** (-0.5) * math.log2(math.e)
    for head in range(local_width // VHD):
        at = slice(head * VHD, (head + 1) * VHD)
        scores = (
            lax.dot_general(
                queries[:, at], keys[:, at], CONTRACT_LAST, preferred_element_type=f32
            )
            + bias
        )
        powered = jnp.exp2((scores - jnp.max(scores, axis=-1, keepdims=True)) * factor)
        total = jnp.sum(powered, axis=-1, keepdims=True)
        mixed = jnp.dot(powered.astype(bf16), values[:, at], preferred_element_type=f32)
        context[:, at] = (mixed / total).astype(bf16)
    row = lax.broadcasted_iota(jnp.int32, (tokens, patch_count), 0)
    column = lax.broadcasted_iota(jnp.int32, (tokens, patch_count), 1)
    pooling = jnp.where(column // POOL == row, 1.0 / POOL, 0.0).astype(bf16)
    pooled = jnp.dot(pooling, context[...], preferred_element_type=f32).astype(bf16)
    own = jnp.dot(pooling, own_ref[0], preferred_element_type=f32)
    attended = jnp.dot(pooled, wout_ref[...], preferred_element_type=f32)
    for part in range(parts):
        block = attended[:, part * part_width : (part + 1) * part_width]
        out_ref[part, 0] = (block + jnp.where(my_ref[0] == part, own, 0.0)).astype(bf16)


def attend(full, own, valid_count, my, ln_gain, w_qkv, w_out):
    parts, frames, patch_count, part_width = full.shape
    width = parts * part_width
    local_width = w_qkv.shape[2]
    tokens = patch_count // POOL
    return pl.pallas_call(
        attend_kernel,
        out_shape=jax.ShapeDtypeStruct((parts, frames, tokens, part_width), bf16),
        grid_spec=pltpu.PrefetchScalarGridSpec(
            num_scalar_prefetch=2,
            grid=(frames,),
            in_specs=[
                pl.BlockSpec((parts, 1, patch_count, part_width), lambda f, *_: (0, f, 0, 0)),
                pl.BlockSpec((1, patch_count, part_width), lambda f, *_: (f, 0, 0)),
                pl.BlockSpec((parts, 1, part_width), lambda f, *_: (0, 0, 0)),
                pl.BlockSpec((3, width, local_width), lambda f, *_: (0, 0, 0)),
                pl.BlockSpec((local_width, width), lambda f, *_: (0, 0)),
            ],
            out_specs=pl.BlockSpec((parts, 1, tokens, part_width), lambda f, *_: (0, f, 0, 0)),
            scratch_shapes=[
                VMEM((patch_count, width), bf16),
                VMEM((patch_count, local_width), bf16),
            ],
        ),
        name="attend",
    )(valid_count, my, full, own, ln_gain.reshape(parts, 1, part_width), w_qkv, w_out)


def bucket_kernel(slot_ref, label_ref, count_ref, parts_ref, out_ref):
    parts, _, tokens, part_width = parts_ref.shape
    padded = out_ref.shape[2]
    spot = lax.broadcasted_iota(jnp.int32, (tokens, part_width), 0) * POOL

    def step(target, carry):
        slot = slot_ref[target]
        total = sum(parts_ref[part, slot].astype(f32) for part in range(parts))
        kept = jnp.where(spot < count_ref[target], total, 0.0)
        out_ref[target, :, :part_width] = kept.astype(bf16)
        out_ref[target, :, part_width:] = jnp.full(
            (tokens, padded - part_width), label_ref[target].astype(f32)
        ).astype(bf16)
        return carry

    lax.fori_loop(0, out_ref.shape[0], step, 0)


def bucket(parts, frame_ids, valid_count, shards):
    frames, tokens, part_width = parts.shape[1:]
    padded = (part_width // LANES + 1) * LANES
    onehot = (frame_ids // frames)[None, :] == jnp.arange(shards)[:, None]
    pick = lambda row: jnp.sum(jnp.where(onehot, row[None, :], 0), axis=1).astype(jnp.int32)
    return pl.pallas_call(
        bucket_kernel,
        out_shape=jax.ShapeDtypeStruct((shards, tokens, padded), bf16),
        in_specs=[pl.BlockSpec(memory_space=pltpu.SMEM)] * 3 + [pl.BlockSpec(memory_space=VMEM)],
        out_specs=pl.BlockSpec(memory_space=VMEM),
        name="bucket",
    )(
        pick(jnp.arange(frames, dtype=jnp.int32)),
        pick(frame_ids % frames + 1),
        pick(valid_count),
        parts,
    )


def connect_kernel(
    sender_ref, my_ref, arrived_ref, weight_ref, gain_ref, stream_ref, normed_ref, rows, wide
):
    parts, _, tokens, _ = arrived_ref.shape
    width, columns = weight_ref.shape[1:]
    part_width = width // parts
    block_frames = rows.shape[0] // tokens
    for spot in range(block_frames):
        sender = sender_ref[pl.program_id(0) * block_frames + spot]
        for part in range(parts):
            rows[
                spot * tokens : (spot + 1) * tokens, part * part_width : (part + 1) * part_width
            ] = arrived_ref[part, sender, :, :part_width]
    squares = 0.0
    for part in range(parts):
        piece = jnp.dot(rows[...], weight_ref[part], preferred_element_type=f32).astype(bf16)

        @pl.when(my_ref[0] == part)
        def _():
            stream_ref[...] = piece

        piece = piece.astype(f32)
        wide[:, part * columns : (part + 1) * columns] = piece
        squares = squares + jnp.sum(piece * piece, axis=-1, keepdims=True)
    scale = lax.rsqrt(squares / (parts * columns) + 1e-05)
    normed_ref[...] = (wide[...] * scale * gain_ref[...]).astype(bf16)


def connect(arrived, senders, my, weights, norm_gain):
    parts, shards, tokens, padded = arrived.shape
    width, columns = weights.shape[1:]
    frames = senders.shape[0]
    block = math.gcd(frames, 4)
    return pl.pallas_call(
        connect_kernel,
        out_shape=(
            jax.ShapeDtypeStruct((frames * tokens, columns), bf16),
            jax.ShapeDtypeStruct((frames * tokens, parts * columns), bf16),
        ),
        grid_spec=pltpu.PrefetchScalarGridSpec(
            num_scalar_prefetch=2,
            grid=(frames // block,),
            in_specs=[
                pl.BlockSpec((parts, shards, tokens, padded), lambda i, *_: (0, 0, 0, 0)),
                pl.BlockSpec((parts, width, columns), lambda i, *_: (0, 0, 0)),
                pl.BlockSpec((1, parts * columns), lambda i, *_: (0, 0)),
            ],
            out_specs=(
                pl.BlockSpec((block * tokens, columns), lambda i, *_: (i, 0)),
                pl.BlockSpec((block * tokens, parts * columns), lambda i, *_: (i, 0)),
            ),
            scratch_shapes=[
                VMEM((block * tokens, width), bf16),
                VMEM((block * tokens, parts * columns), f32),
            ],
        ),
        name="connect",
    )(senders, my, arrived, weights, norm_gain.reshape(1, -1))


def paired(columns, pair, rows):
    lane = lax.broadcasted_iota(jnp.int32, (rows, LANES), 1)
    return jnp.where(
        lane < HDIM, columns[:, 2 * pair : 2 * pair + 1], columns[:, 2 * pair + 1 : 2 * pair + 2]
    )


def final_state_kernel(inner_ref, write_ref, weight_ref, out_ref):
    length, features = inner_ref.shape
    weights = weight_ref[0]
    for pair in range(features // LANES):
        at = slice(pair * LANES, (pair + 1) * LANES)
        scaled = (inner_ref[:, at].astype(f32) * paired(weights, pair, length)).astype(bf16)
        out_ref[at, :] = lax.dot_general(
            scaled, write_ref[...], CONTRACT_FIRST, preferred_element_type=f32
        ).astype(bf16)


def final_state(inner, write, weights):
    length = inner.shape[0]
    groups = weights.shape[0]
    features = inner.shape[1] // groups
    return pl.pallas_call(
        final_state_kernel,
        out_shape=jax.ShapeDtypeStruct((groups * features, STATE), bf16),
        grid=(groups,),
        in_specs=[
            pl.BlockSpec((length, features), lambda g: (0, g)),
            pl.BlockSpec((length, STATE), lambda g: (0, g)),
            pl.BlockSpec((1, length, weights.shape[2]), lambda g: (g, 0, 0)),
        ],
        out_specs=pl.BlockSpec((features, STATE), lambda g: (g, 0)),
        name="final_state",
    )(inner, write, weights)


def local_kernel(
    inner_ref, write_ref, read_ref, down_ref, across_ref, step_ref, left_ref, skip_ref, out_ref, state
):
    length, features = inner_ref.shape

    @pl.when(pl.program_id(1) == 0)
    def _():
        state[...] = jnp.zeros_like(state)

    readers, writers = read_ref[...], write_ref[...]
    crossing = lax.dot_general(readers, writers, CONTRACT_LAST, preferred_element_type=f32)
    causal = lax.broadcasted_iota(jnp.int32, (length, length), 0) >= lax.broadcasted_iota(
        jnp.int32, (length, length), 1
    )
    crossing = jnp.where(causal, crossing, 0.0)
    down, across, steps, left = down_ref[0], across_ref[0], step_ref[0], left_ref[0]
    grown = jnp.exp(down)
    lane = lax.broadcasted_iota(jnp.int32, (length, LANES), 1)
    row = lax.broadcasted_iota(jnp.int32, (LANES, STATE), 0)
    for pair in range(features // LANES):
        at = slice(pair * LANES, (pair + 1) * LANES)
        inner = inner_ref[:, at]
        halves = []
        for head in (2 * pair, 2 * pair + 1):
            spans = jnp.minimum(down[:, head : head + 1] - across[head : head + 1, :], 0.0)
            mixing = crossing * jnp.exp(spans) * steps[head : head + 1, :]
            halves.append(jnp.dot(mixing.astype(bf16), inner, preferred_element_type=f32))
        held = state[at, :]
        carried = lax.dot_general(
            readers, held.astype(bf16), CONTRACT_LAST, preferred_element_type=f32
        )
        inner = inner.astype(f32)
        out_ref[:, at] = (
            jnp.where(lane < HDIM, halves[0], halves[1])
            + carried * paired(grown, pair, length)
            + skip_ref[:, at] * inner
        )
        scaled = (inner * paired(left, pair, length)).astype(bf16)
        last = grown[length - 1 :, :]
        faded = held * jnp.where(
            row < HDIM, last[:, 2 * pair : 2 * pair + 1], last[:, 2 * pair + 1 : 2 * pair + 2]
        )
        state[at, :] = faded + lax.dot_general(
            scaled, writers, CONTRACT_FIRST, preferred_element_type=f32
        )


def local_outputs(inner, write, read, down, across, steps, left, skip):
    length = inner.shape[0]
    groups, _, per_group = down.shape
    features = inner.shape[1] // groups
    tall = pl.BlockSpec((1, CHUNK, per_group), lambda g, c: (g, c, 0))
    flat = pl.BlockSpec((1, per_group, CHUNK), lambda g, c: (g, 0, c))
    return pl.pallas_call(
        local_kernel,
        out_shape=jax.ShapeDtypeStruct(inner.shape, f32),
        grid=(groups, length // CHUNK),
        in_specs=[
            pl.BlockSpec((CHUNK, features), lambda g, c: (c, g)),
            pl.BlockSpec((CHUNK, STATE), lambda g, c: (c, g)),
            pl.BlockSpec((CHUNK, STATE), lambda g, c: (c, g)),
            tall,
            flat,
            flat,
            tall,
            pl.BlockSpec((1, features), lambda g, c: (0, g)),
        ],
        out_specs=pl.BlockSpec((CHUNK, features), lambda g, c: (c, g)),
        scratch_shapes=[VMEM((features, STATE), f32)],
        cost_estimate=pl.CostEstimate(
            flops=20_000_000_000, bytes_accessed=20_000_000, transcendentals=4_000_000
        ),
        name="local_outputs",
    )(inner, write, read, down, across, steps, left, skip)


def prefix_kernel(arrived_ref, decay_ref, out_ref):
    shards, rows, _ = out_ref.shape
    current = jnp.zeros(out_ref.shape[1:], f32)
    for shard in range(shards):
        out_ref[shard] = current.astype(bf16)
        current = decay_ref[shard] * current + arrived_ref[shard, :rows].astype(f32)


def incoming_state(state, row_log, shards):
    rows = state.shape[0] // shards
    room = 8 * LANES
    logs = row_log.reshape(shards, rows)
    high = logs.astype(bf16)
    low = (logs - high.astype(f32)).astype(bf16)
    widen = lambda part: jnp.pad(part, ((0, 0), (0, room - rows))).reshape(shards, 8, LANES)
    outgoing = jnp.concatenate(
        [state.reshape(shards, rows, STATE), widen(high), widen(low)], axis=1
    )
    arrived = lax.all_to_all(outgoing, "tm", split_axis=0, concat_axis=0, tiled=True)
    tail = arrived[:, rows:].astype(f32).reshape(shards, 2, room)[:, :, :rows]
    decay = jnp.exp(tail[:, 0] + tail[:, 1])[:, :, None]
    before = pl.pallas_call(
        prefix_kernel,
        out_shape=jax.ShapeDtypeStruct((shards, rows, STATE), bf16),
        in_specs=[pl.BlockSpec(memory_space=VMEM)] * 2,
        out_specs=pl.BlockSpec(memory_space=VMEM),
        name="prefix",
    )(arrived, decay)
    return lax.all_to_all(before, "tm", split_axis=0, concat_axis=0, tiled=True).reshape(
        shards * rows, STATE
    )


def finish_kernel(local_ref, read_ref, state_ref, grown_ref, gain_ref, out_ref, total):
    length, features = local_ref.shape
    grown = grown_ref[0]
    squares = 0.0
    for pair in range(features // LANES):
        at = slice(pair * LANES, (pair + 1) * LANES)
        carried = lax.dot_general(
            read_ref[...], state_ref[at, :], CONTRACT_LAST, preferred_element_type=f32
        )
        summed = local_ref[:, at] + carried * paired(grown, pair, length)
        total[:, at] = summed
        squares = squares + jnp.sum(summed * summed, axis=-1, keepdims=True)
    scale = lax.rsqrt(squares / features + 1e-05)
    out_ref[...] = (total[...] * scale * gain_ref[...]).astype(bf16)


def finish(local, read, state, grown, out_gain):
    length = local.shape[0]
    groups, _, per_group = grown.shape
    features = local.shape[1] // groups
    block = 2 * CHUNK
    return pl.pallas_call(
        finish_kernel,
        out_shape=jax.ShapeDtypeStruct(local.shape, bf16),
        grid=(groups, length // block),
        in_specs=[
            pl.BlockSpec((block, features), lambda g, c: (c, g)),
            pl.BlockSpec((block, STATE), lambda g, c: (c, g)),
            pl.BlockSpec((features, STATE), lambda g, c: (g, 0)),
            pl.BlockSpec((1, block, per_group), lambda g, c: (g, c, 0)),
            pl.BlockSpec((1, features), lambda g, c: (0, g)),
        ],
        out_specs=pl.BlockSpec((block, features), lambda g, c: (c, g)),
        scratch_shapes=[VMEM((block, features), f32)],
        name="finish",
    )(local, read, state, grown, out_gain.reshape(1, -1))


def on_device(
    patches,
    grid_rows,
    frame_ids,
    ln_gain,
    w_qkv,
    w_out,
    w_conn,
    norm_gain,
    w_x,
    w_b,
    w_c,
    w_dt,
    dt_bias,
    a_log,
    d_skip,
    out_gain,
):
    frame_count, patch_count, part_width = patches.shape
    shards = lax.axis_size("tm")
    my = lax.axis_index("head").astype(jnp.int32).reshape(1)
    full = lax.all_gather(patches, "head")
    all_conn = lax.all_gather(w_conn, "head")
    valid_count = (grid_rows * GRID).astype(jnp.int32)
    parts = attend(full, patches, valid_count, my, ln_gain, w_qkv, w_out)
    parts = lax.all_to_all(parts, "head", split_axis=0, concat_axis=0, tiled=True)
    outgoing = bucket(parts, frame_ids, valid_count, shards)
    incoming = lax.all_to_all(outgoing, "tm", split_axis=0, concat_axis=0, tiled=True)
    labels = incoming[:, 0, part_width].astype(jnp.int32)
    senders = jnp.sum(
        jnp.where(
            labels[None, :] == jnp.arange(1, frame_count + 1)[:, None],
            jnp.arange(shards, dtype=jnp.int32)[None, :],
            0,
        ),
        axis=1,
    ).astype(jnp.int32)
    arrived = lax.all_gather(incoming, "head")
    stream_rows, normed = connect(arrived, senders, my, all_conn, norm_gain)

    tokens = stream_rows.shape[0]
    heads = w_dt.shape[1]
    groups = w_b.shape[1] // STATE
    per_group = heads // groups
    chunks = tokens // CHUNK
    step_size = jax.nn.softplus(jnp.dot(normed, w_dt, preferred_element_type=f32) + dt_bias)
    log_decay = -jnp.exp(a_log) * step_size
    inner = jnp.dot(normed, w_x, preferred_element_type=f32).astype(bf16)
    write = jnp.dot(normed, w_b, preferred_element_type=f32).astype(bf16)
    read = jnp.dot(normed, w_c, preferred_element_type=f32).astype(bf16)

    cumul = jnp.cumsum(log_decay.reshape(chunks, CHUNK, heads), axis=1)
    ends = cumul[:, -1, :]
    offsets = jnp.cumsum(ends, axis=0) - ends
    total_log = jnp.sum(ends, axis=0)
    from_start = (cumul + offsets[:, None, :]).reshape(tokens, heads)
    tall = lambda member: member.reshape(tokens, groups, per_group).transpose(1, 0, 2)
    flat = lambda member: member.reshape(tokens, groups, per_group).transpose(1, 2, 0)
    state = final_state(inner, write, tall(step_size * jnp.exp(total_log - from_start)))
    before = incoming_state(state, jnp.repeat(total_log, HDIM), shards)
    left = step_size * jnp.exp(ends[:, None, :] - cumul).reshape(tokens, heads)
    local = local_outputs(
        inner,
        write,
        read,
        tall(cumul),
        flat(cumul),
        flat(step_size),
        tall(left),
        jnp.repeat(d_skip, HDIM).reshape(1, -1),
    )
    return stream_rows, finish(local, read, before, tall(jnp.exp(from_start)), out_gain)


def solution(mesh):
    in_specs = (
        P("tm", None, "head"),
        P("tm"),
        P("tm"),
        P(),
        P(None, None, "head"),
        P("head", None),
        P(None, "head"),
        P(),
        P(None, "head"),
        P(None, "head"),
        P(None, "head"),
        P(None, "head"),
        P("head"),
        P("head"),
        P("head"),
        P("head"),
    )
    out_specs = (P("tm", "head"), P("tm", "head"))
    return jax.shard_map(
        on_device, mesh=mesh, in_specs=in_specs, out_specs=out_specs, check_vma=False
    )
```

time: 799 us -> 304 us (0.38); the launches traced: 784 us -> 302 us
  local copies, waits for them, and re-layouts: 267 us -> 34.8 us
  waiting for transfers between devices: 188 us -> 18.6 us
  Pallas kernels: 0 us -> 131 us
  matrix products: 158 us -> 39.3 us
  other arithmetic: 97.4 us -> 5.18 us
    dynamic_update_slice x6 -> x0, local copies, waits for them, and re-layouts: 143 us -> none  [on_device(): device_state, (outputs, cumul) = lax.scan(stretch_step, zero_state, sliced)]
    pallas_call x0 -> x7, Pallas kernels: none -> 131 us  [the longest x1 60 us: attend(): pl.pallas_call(attend_kernel, out_shape=jax.ShapeDtypeStruct((parts, fram...]
    dot_general x23 -> x4, matrix products: 142 us -> 39.3 us  [the longest x1 21.8 us: on_device(): inner = jnp.dot(normed, w_x, preferred_element_type=f32).astype(bf16)]
    all_gather x3, waiting for transfers between devices: 108 us -> 14 us  [the longest x1 7.45 us: on_device(): full = lax.all_gather(patches, 'head')]
    all_to_all x2, waiting for transfers between devices: 79.3 us -> 3.2 us  [the longest x1 3.2 us: incoming_state(): lax.all_to_all(outgoing, 'tm', split_axis=0, concat_axis=0, tiled=True)]
    all_to_all x0 -> x2, blocking collectives: none -> 48.1 us  [the longest x1 39.7 us: on_device(): lax.all_to_all(outgoing, 'tm', split_axis=0, concat_axis=0, tiled=True)]
    unnamed x1 -> x0, blocking collectives: 42.8 us -> none
    reduce_sum x8 -> x3, other arithmetic: 34.5 us -> 1.4 us  [the longest x1 0.7 us: on_device(): jnp.sum(jnp.where(labels[None, :] == jnp.arange(1, frame_count + 1)[:, No...]
  transfers between devices with their start and end apart: 6 -> 5, of which waited for: 4 -> 3; matrix products, arithmetic and copies ran while one was open for 8% -> 14% of each run, Pallas kernels for 0% -> 29%
where the time goes in v1:
time: 304 us; the launch traced here: 302 us
  Pallas kernels  131 us (43%)
  blocking collectives  48.1 us (16%)
  matrix products  39.3 us (13%)
  local copies, waits for them, and re-layouts  34.8 us (11%)
  waiting for transfers between devices  18.6 us (6%)
  between operations  14 us (5%)
  starting transfers between devices  11.2 us (4%)
  other arithmetic  5.18 us (2%)
    pallas_call x1, Pallas kernels, attend(): pl.pallas_call(attend_kernel, out_shape=jax.ShapeDtypeStruct((parts, fram...  60 us
    all_to_all x1, blocking collectives, on_device(): lax.all_to_all(outgoing, 'tm', split_axis=0, concat_axis=0, tiled=True)  39.7 us
    pallas_call x1, Pallas kernels, local_outputs(): pl.pallas_call(local_kernel, out_shape=jax.ShapeDtypeStruct(inner.shape,...  25.1 us
    dot_general x1, matrix products, on_device(): inner = jnp.dot(normed, w_x, preferred_element_type=f32).astype(bf16)  21.8 us
    pallas_call x1, Pallas kernels, connect(): pl.pallas_call(connect_kernel, out_shape=(jax.ShapeDtypeStruct((frames *...  19.1 us
    unnamed x39, local copies, waits for them, and re-layouts  13.7 us
    pallas_call x1, Pallas kernels, finish(): pl.pallas_call(finish_kernel, out_shape=jax.ShapeDtypeStruct(local.shape,...  13.3 us
    all_gather x1, local copies, waits for them, and re-layouts, on_device(): full = lax.all_gather(patches, 'head')  10.7 us
  transfers between devices with their start and end apart: 5, of which 3 were waited for; matrix products, arithmetic and copies ran while one was open for 14% of the time, Pallas kernels for 29%

profile of v1, /device:TPU:0, one launch (start us, length us, event | category | flops | bytes accessed | tf_op | source)
XLA Modules:
  0.0 301.7 jit_solution(13266439772274708691)
XLA Ops:
  7.2 0.0 copy-start
  7.2 0.0 all-gather.7.cloned.1.call-start
  7.2 0.7 all-gather.7.cloned.1.call-update
  7.9 0.0 all-gather.11.cloned.1.call-start
  8.0 0.7 all-gather.11.cloned.1.call-update
  8.7 0.0 all-gather.9.cloned.1.call-start
  8.7 6.0 %copy.68.own_ref = bf16[12,256,576]{2,1,0:T(8,128)(2,1)} copy(bf16[12,256,576]{1,2,0:T(8,128)(2,1)} %param.16) | data formatting | bytes 7077888 | tf_op args[0]
  14.7 6.7 %copy.69.wqkv_ref = bf16[3,1152,576]{2,1,0:T(8,128)(2,1)} copy(bf16[3,1152,576]{1,2,0:T(8,128)(2,1)} %param.20) | data formatting | bytes 7962624 | tf_op args[4]
  21.4 0.0 copy-done.6
  21.4 0.7 reshape.107.gain_ref
  22.0 0.0 copy-done.11
  22.1 0.0 copy-done.12
  22.1 0.7 select_reduce_fusion.1
  22.8 7.4 %all-gather.7.cloned.1.call-done = bf16[24,256,576]{1,2,0:T(8,128)(2,1)} async-done(((bf16[12,256,576]{1,2,0:T(8,128)(2,1)}), bf16[24,256,576]{1,2,0:T(8,128)(2,1)}) %all-gather.7.cloned.1.call-update) | async-done | bytes 7077904 | tf_op jit(solution)/shard_map/all_gather | solution.py:403
  30.2 10.7 %copy.67 = bf16[24,256,576]{2,1,0:T(8,128)(2,1)} copy(bf16[24,256,576]{1,2,0:T(8,128)(2,1)} %all-gather.7.cloned.1.call-done) | data formatting | bytes 14155776 | tf_op jit(solution)/shard_map/all_gather | solution.py:403
  40.9 0.0 copy-done.7
  40.9 60.0 %attend.1 = bf16[2,12,64,576]{3,2,1,0:T(8,128)(2,1)} custom-call(s32[12]{0:T(128)} %copy-done.7, s32[1]{0:T(128)} %bitcast.my_ref, bf16[2,12,256,576]{3,2,1,0:T(8,128)(2,1)} %bitcast.47, bf16[12,256,576]{2,1,0:T(8,128)(2,1)} %copy.68.own_ref, f32[2,1,576]{2,1,0:T(1,128)} %reshape.107.gain_ref, bf16[3,1152,576]{2,1,0:T(8,128)(2,1)} %copy.69.wqkv_ref, ...), custom_call_target="tpu_custom_call" | custom-call | tf_op jit(solution)/shard_map/attend/pallas_call | solution.py:79
  100.9 8.4 %all_to_all.20.parts_ref = bf16[2,12,64,576]{3,2,1,0:T(8,128)(2,1)} all-to-all(bf16[2,12,64,576]{3,2,1,0:T(8,128)(2,1)} %attend.1), channel_id=1, replica_groups=mesh['tm'=16,'head'=2] {'head'}, dimensions={0} | all-to-all | bytes 3538944 | tf_op jit(solution)/shard_map/all_to_all | solution.py:407
  109.2 3.2 %bucket.1 = bf16[16,64,640]{2,1,0:T(8,128)(2,1)} custom-call(s32[16]{0:T(128)} %get-tuple-element.8.slot_ref, s32[16]{0:T(128)} %get-tuple-element.7.label_ref, s32[16]{0:T(128)} %get-tuple-element.6.count_ref, bf16[2,12,64,576]{3,2,1,0:T(8,128)(2,1)} %all_to_all.20.parts_ref), custom_call_target="tpu_custom_call" | custom-call | tf_op jit(solution)/shard_map/bucket/pallas_call | solution.py:125
  112.4 39.7 %all_to_all.21 = bf16[16,64,640]{2,1,0:T(8,128)(2,1)} all-to-all(bf16[16,64,640]{2,1,0:T(8,128)(2,1)} %bucket.1), channel_id=1, replica_groups=mesh['tm'=16,'head'=2] {'tm'}, dimensions={0} | all-to-all | bytes 2621440 | tf_op jit(solution)/shard_map/all_to_all | solution.py:409
  152.1 0.0 all-gather.9.cloned.1.call-update
  152.2 0.0 copy-done.9
  152.2 0.1 broadcast_in_dim.65
  152.2 0.7 reshape_reshape.4.skip_ref
  152.9 0.0 copy-done.13
  152.9 1.2 fusion.1
  154.2 0.7 select_reduce_fusion.sender_ref
  154.9 6.6 %all-gather.9.cloned.1.call-done = bf16[32,64,640]{2,1,0:T(8,128)(2,1)} async-done(((bf16[16,64,640]{2,1,0:T(8,128)(2,1)}), bf16[32,64,640]{2,1,0:T(8,128)(2,1)}) %all-gather.9.cloned.1.call-update) | async-done | bytes 2621456 | tf_op jit(solution)/shard_map/all_gather | solution.py:419
  161.4 19.1 %connect.1 = (bf16[768,2048]{1,0:T(8,128)(2,1)}, bf16[768,4096]{1,0:T(8,128)(2,1)}) custom-call(s32[12]{0:T(128)} %select_reduce_fusion.sender_ref, s32[1]{0:T(128)} %bitcast.my_ref, bf16[2,16,64,640]{3,2,1,0:T(8,128)(2,1)} %bitcast.53, bf16[2,1152,2048]{2,1,0:T(8,128)(2,1)} %bitcast.48, f32[1,4096]{1,0:T(1,128)} %bitcast.67), custom_call_target="tpu_custom_call" | custom-call | tf_op jit(solution)/shard_map/connect/pallas_call | solution.py:172
  180.5 4.8 %broadcast_multiply_fusion = (f32[768,32]{0,1:T(8,128)S(1)}, f32[768,32]{0,1:T(8,128)S(1)}) fusion(f32[32]{0:T(128)S(1)} %exponential_negate_fusion, f32[32]{0:T(128)S(1)} %copy-done.8, bf16[768,4096]{1,0:T(8,128)(2,1)} %get-tuple-element.5, bf16[4096,32]{0,1:T(8,128)(2,1)S(1)} %copy-done), kind=kOutput, calls=%fused_computation.13 | convolution fusion | flops 201523200 | bytes 6750464 | tf_op jit(solution)/shard_map/dot_general | solution.py:427
  185.3 0.0 copy-start.5
  185.4 0.2 copy.80
  185.5 0.4 reduce_window_sum.22
  185.9 0.2 copy.71
  186.1 0.1 copy.86
  186.2 0.1 broadcast_add_fusion
  186.3 0.1 copy.81
  186.4 0.1 copy.82
  186.6 0.1 broadcast_in_dim.66
  186.7 0.1 multiply_bitcast_fusion
  186.8 0.0 slice-start
  186.8 1.6 copy.76
  188.4 21.8 %convolution_convert_fusion.inner_ref = bf16[768,2048]{1,0:T(8,128)(2,1)} fusion(bf16[768,4096]{1,0:T(8,128)(2,1)} %get-tuple-element.5, bf16[4096,2048]{1,0:T(8,128)(2,1)} %param.24), kind=kOutput, calls=%fused_computation | convolution fusion | flops 12886474752 | bytes 26214400 | tf_op jit(solution)/shard_map/dot_general | solution.py:429
  210.3 4.3 %convolution_convert_fusion.2.write_ref = bf16[768,512]{1,0:T(8,128)(2,1)} fusion(bf16[768,4096]{1,0:T(8,128)(2,1)S(1)} %bitcast.50, bf16[4096,512]{1,0:T(8,128)(2,1)S(1)} %copy-done.10), kind=kOutput, calls=%fused_computation.2 | convolution fusion | flops 3221618688 | bytes 11272192 | tf_op jit(solution)/shard_map/dot_general | solution.py:430
  214.7 0.1 broadcast_in_dim.67
  214.7 0.1 broadcast_in_dim.68
  214.9 7.4 %final_state.1 = bf16[2048,128]{1,0:T(8,128)(2,1)} custom-call(bf16[768,2048]{1,0:T(8,128)(2,1)} %convolution_convert_fusion.inner_ref, bf16[768,512]{1,0:T(8,128)(2,1)} %convolution_convert_fusion.2.write_ref, f32[4,768,8]{2,1,0:T(8,128)} %bitcast.51), custom_call_target="tpu_custom_call" | custom-call | tf_op jit(solution)/shard_map/final_state/pallas_call | solution.py:221
  222.3 1.9 pad_maximum_fusion
  224.2 6.8 %all-to-all-start.2 = ((bf16[16,144,128]{2,1,0:T(8,128)(2,1)}), bf16[16,144,128]{2,1,0:T(8,128)(2,1)S(1)}, u32[]{:S(2)}, u32[]{:S(2)}) async-start(bf16[16,144,128]{2,1,0:T(8,128)(2,1)} %pad_maximum_fusion), calls=%async_computation.2 | async-start | bytes 1179648 | tf_op jit(solution)/shard_map/all_to_all | solution.py:329
  231.0 1.6 copy.74
  232.6 1.7 copy.72
  234.3 0.1 add.70.clone
  234.5 1.6 copy.79
  236.1 8.3 %convolution_convert_fusion.1.read_ref = bf16[768,512]{1,0:T(8,128)(2,1)} fusion(bf16[768,4096]{1,0:T(8,128)(2,1)} %get-tuple-element.5, bf16[4096,512]{1,0:T(8,128)(2,1)} %param.26), kind=kOutput, calls=%fused_computation.1 | convolution fusion | flops 3221618688 | bytes 11272192 | tf_op jit(solution)/shard_map/dot_general | solution.py:431
  244.4 3.2 %all-to-all-done.2.arrived_ref = bf16[16,144,128]{2,1,0:T(8,128)(2,1)S(1)} async-done(((bf16[16,144,128]{2,1,0:T(8,128)(2,1)}), bf16[16,144,128]{2,1,0:T(8,128)(2,1)S(1)}, u32[]{:S(2)}, u32[]{:S(2)}) %all-to-all-start.2) | async-done | bytes 589856 | tf_op jit(solution)/shard_map/all_to_all | solution.py:329
  247.6 0.1 reshape.123
  247.7 1.4 copy.77.decay_ref
  249.1 2.5 prefix.1
  251.6 4.3 %all-to-all-start.3 = ((bf16[16,128,128]{2,1,0:T(8,128)(2,1)}), bf16[16,128,128]{2,1,0:T(8,128)(2,1)S(1)}, u32[]{:S(2)}, u32[]{:S(2)}) async-start(bf16[16,128,128]{2,1,0:T(8,128)(2,1)} %prefix.1), calls=%async_computation.3 | async-start | bytes 1048576 | tf_op jit(solution)/shard_map/all_to_all | solution.py:339
  255.9 25.1 %local_outputs.1.local_ref = f32[768,2048]{1,0:T(8,128)} custom-call(bf16[768,2048]{1,0:T(8,128)(2,1)} %convolution_convert_fusion.inner_ref, bf16[768,512]{1,0:T(8,128)(2,1)} %convolution_convert_fusion.2.write_ref, bf16[768,512]{1,0:T(8,128)(2,1)} %convolution_convert_fusion.1.read_ref, f32[4,768,8]{2,1,0:T(8,128)} %bitcast.57, f32[4,8,768]{2,1,0:T(8,128)} %bitcast.61, ...), custom_call_target="tpu_custom_call" | custom-call | flops 20000000000 | bytes 20000000 | tf_op jit(solution)/shard_map/local_outputs/pallas_call | solution.py:288
  281.0 0.0 all-to-all-done.3
  281.0 0.0 copy-start.1
  281.0 0.8 copy-done.3
  281.9 13.3 %finish.1 = bf16[768,2048]{1,0:T(8,128)(2,1)} custom-call(f32[768,2048]{1,0:T(8,128)} %local_outputs.1.local_ref, bf16[768,512]{1,0:T(8,128)(2,1)} %convolution_convert_fusion.1.read_ref, bf16[2048,128]{1,0:T(8,128)(2,1)} %bitcast.55, f32[4,768,8]{2,1,0:T(8,128)} %bitcast.52, f32[1,2048]{1,0:T(1,128)} %bitcast.68), custom_call_target="tpu_custom_call" | custom-call | tf_op jit(solution)/shard_map/finish/pallas_call | solution.py:365
  (39 shorter events, 0.2 us)
Async XLA Ops:
  7.2 173.4 %copy-start = (bf16[4096,32]{0,1:T(8,128)(2,1)S(1)}, bf16[4096,32]{0,1:T(8,128)(2,1)}, u32[]{:S(2)}) copy-start(bf16[4096,32]{0,1:T(8,128)(2,1)} %param.27) | copy-start | bytes 786436
  7.2 23.0 %all-gather.7.cloned.1.call-start = ((), (), s32[]{:S(2)}) async-start(), calls=%async_computation.4 | async-start | bytes 10616832 | tf_op jit(solution)/shard_map/all_gather | solution.py:403
  7.9 146.9 %all-gather.11.cloned.1.call-start = ((), (), s32[]{:S(2)}) async-start(), calls=%async_computation.6 | async-start | bytes 14155776 | tf_op jit(solution)/shard_map/all_gather | solution.py:404
  8.7 152.8 %all-gather.9.cloned.1.call-start = ((), (), s32[]{:S(2)}) async-start(), calls=%async_computation.5 | async-start | bytes 3932160 | tf_op jit(solution)/shard_map/all_gather | solution.py:419
  14.7 6.7 %copy-start.6 = (f32[1152]{0:T(1024)S(1)}, f32[1152]{0:T(1024)}, u32[]{:S(2)}) copy-start(f32[1152]{0:T(1024)} %param.19) | copy-start | bytes 13828
  14.7 7.4 %copy-start.11 = (s32[12]{0:T(128)S(1)}, s32[12]{0:T(128)}, u32[]{:S(2)}) copy-start(s32[12]{0:T(128)} %param.17) | copy-start | bytes 148
  14.7 7.4 %copy-start.12 = (s32[12]{0:T(128)S(1)}, s32[12]{0:T(128)}, u32[]{:S(2)}) copy-start(s32[12]{0:T(128)} %param.18) | copy-start | bytes 148
  22.1 18.8 %copy-start.7 = (s32[12]{0:T(128)}, s32[12]{0:T(128)S(1)}, u32[]{:S(2)}) copy-start(s32[12]{0:T(128)S(1)} %broadcast_multiply_fusion.1.valid_ref) | copy-start | bytes 148
  109.2 42.9 %copy-start.9 = (f32[32]{0:T(128)S(1)}, f32[32]{0:T(128)}, u32[]{:S(2)}) copy-start(f32[32]{0:T(128)} %param.30) | copy-start | bytes 388
  109.2 43.7 %copy-start.13 = (f32[32]{0:T(128)S(1)}, f32[32]{0:T(128)}, u32[]{:S(2)}) copy-start(f32[32]{0:T(128)} %param.29) | copy-start | bytes 388
  161.4 19.1 %copy-start.8 = (f32[32]{0:T(128)S(1)}, f32[32]{0:T(128)}, u32[]{:S(2)}) copy-start(f32[32]{0:T(128)} %param.28) | copy-start | bytes 388
  185.3 24.9 %copy-start.5 = (f32[768,32]{0,1:T(8,128)}, f32[768,32]{0,1:T(8,128)S(1)}, u32[]{:S(2)}) copy-start(f32[768,32]{0,1:T(8,128)S(1)} %get-tuple-element.20) | copy-start | bytes 294916
  186.8 23.5 %slice-start = ((s8[6291456]{0:T(1024)(128)(4,1)}), s8[2097152]{0:T(1024)(128)(4,1)S(1)}, s32[]{:S(2)}) async-start(s8[6291456]{0:T(1024)(128)(4,1)} %bitcast.49), calls=%async_computation.7 | async-start | bytes 4194304
  188.4 21.9 %slice-start.1 = ((s8[6291456]{0:T(1024)(128)(4,1)}), s8[4194304]{0:T(1024)(128)(4,1)S(1)}, s32[]{:S(2)}) async-start(s8[6291456]{0:T(1024)(128)(4,1)} %bitcast.49), calls=%async_computation.8 | async-start | bytes 8388608
  188.4 21.9 %copy-start.10 = (bf16[4096,512]{1,0:T(8,128)(2,1)S(1)}, bf16[4096,512]{1,0:T(8,128)(2,1)}, u32[]{:S(2)}) copy-start(bf16[4096,512]{1,0:T(8,128)(2,1)} %param.25) | copy-start | bytes 12582916
  224.2 23.4 %all-to-all-start.2 = ((bf16[16,144,128]{2,1,0:T(8,128)(2,1)}), bf16[16,144,128]{2,1,0:T(8,128)(2,1)S(1)}, u32[]{:S(2)}, u32[]{:S(2)}) async-start(bf16[16,144,128]{2,1,0:T(8,128)(2,1)} %pad_maximum_fusion), calls=%async_computation.2 | async-start | bytes 1179648 | tf_op jit(solution)/shard_map/all_to_all | solution.py:329
  232.6 11.8 %copy-start.4 = (f32[768,4,8]{0,2,1:T(8,128)}, f32[768,4,8]{0,2,1:T(8,128)S(1)}, u32[]{:S(2)}) copy-start(f32[768,4,8]{0,2,1:T(8,128)S(1)} %reshape.110) | copy-start | bytes 294916
  247.6 1.5 copy-start.2
  251.6 29.4 %all-to-all-start.3 = ((bf16[16,128,128]{2,1,0:T(8,128)(2,1)}), bf16[16,128,128]{2,1,0:T(8,128)(2,1)S(1)}, u32[]{:S(2)}, u32[]{:S(2)}) async-start(bf16[16,128,128]{2,1,0:T(8,128)(2,1)} %prefix.1), calls=%async_computation.3 | async-start | bytes 1048576 | tf_op jit(solution)/shard_map/all_to_all | solution.py:339
  281.0 0.8 copy-start.3
  281.0 14.2 %copy-start.1 = (bf16[4096,32]{0,1:T(8,128)(2,1)S(1)}, bf16[4096,32]{0,1:T(8,128)(2,1)}, u32[]{:S(2)}) copy-start(bf16[4096,32]{0,1:T(8,128)(2,1)} %param.27) | copy-start | bytes 786436
Sparse Core Ops, SparseCore 0:
  9.5 20.6 all-gather.6
  31.8 22.7 all-gather.10
  152.3 9.0 all-gather.8

commit v2 on v1

--- a/solution.py
+++ b/solution.py
@@ -24,57 +24,65 @@
 
 
 def attend_kernel(
-    valid_ref, my_ref, full_ref, own_ref, gain_ref, wqkv_ref, wout_ref, out_ref, normed, context
+    valid_ref, my_ref, full_ref, gain_ref, wqkv_ref, wout_ref, out_ref, normed, context
 ):
-    parts, _, patch_count, part_width = full_ref.shape
+    parts, _, part_width, patch_count = full_ref.shape
     full_width = parts * part_width
-    local_width = wqkv_ref.shape[2]
+    local_width = wqkv_ref.shape[1]
     tokens = patch_count // POOL
     frame = pl.program_id(0)
     pieces = [full_ref[part, 0].astype(f32) for part in range(parts)]
-    centre = sum(jnp.sum(piece, axis=-1, keepdims=True) for piece in pieces) / full_width
+    centre = sum(jnp.sum(piece, axis=0, keepdims=True) for piece in pieces) / full_width
     pieces = [piece - centre for piece in pieces]
-    spread = sum(jnp.sum(piece * piece, axis=-1, keepdims=True) for piece in pieces) / full_width
+    spread = sum(jnp.sum(piece * piece, axis=0, keepdims=True) for piece in pieces) / full_width
     scale = lax.rsqrt(spread + 1e-06)
     for part in range(parts):
-        normed[:, part * part_width : (part + 1) * part_width] = (
+        normed[part * part_width : (part + 1) * part_width, :] = (
             pieces[part] * scale * gain_ref[part]
         ).astype(bf16)
     rows = normed[...]
     queries, keys, values = [
-        jnp.dot(rows, wqkv_ref[member], preferred_element_type=f32).astype(bf16)
-        for member in range(3)
+        jnp.dot(wqkv_ref[member], rows, preferred_element_type=f32) for member in range(3)
     ]
-    key_spot = lax.broadcasted_iota(jnp.int32, (1, patch_count), 1)
+    key_spot = lax.broadcasted_iota(jnp.int32, (patch_count, patch_count), 0)
     bias = jnp.where(key_spot < valid_ref[frame], 0.0, -1e30).astype(f32)
     factor = VHD ** (-0.5) * math.log2(math.e)
     for head in range(local_width // VHD):
         at = slice(head * VHD, (head + 1) * VHD)
         scores = (
             lax.dot_general(
-                queries[:, at], keys[:, at], CONTRACT_LAST, preferred_element_type=f32
+                keys[at].astype(bf16),
+                queries[at].astype(bf16),
+                CONTRACT_FIRST,
+                preferred_element_type=f32,
             )
             + bias
         )
-        powered = jnp.exp2((scores - jnp.max(scores, axis=-1, keepdims=True)) * factor)
-        total = jnp.sum(powered, axis=-1, keepdims=True)
-        mixed = jnp.dot(powered.astype(bf16), values[:, at], preferred_element_type=f32)
-        context[:, at] = (mixed / total).astype(bf16)
+        powered = jnp.exp2((scores - jnp.max(scores, axis=0, keepdims=True)) * factor)
+        total = jnp.sum(powered, axis=0, keepdims=True)
+        mixed = jnp.dot(
+            values[at].astype(bf16), powered.astype(bf16), preferred_element_type=f32
+        )
+        context[at, :] = mixed / total
     row = lax.broadcasted_iota(jnp.int32, (tokens, patch_count), 0)
     column = lax.broadcasted_iota(jnp.int32, (tokens, patch_count), 1)
     pooling = jnp.where(column // POOL == row, 1.0 / POOL, 0.0).astype(bf16)
-    pooled = jnp.dot(pooling, context[...], preferred_element_type=f32).astype(bf16)
-    own = jnp.dot(pooling, own_ref[0], preferred_element_type=f32)
+    pooled = lax.dot_general(
+        pooling, context[...].astype(bf16), CONTRACT_LAST, preferred_element_type=f32
+    ).astype(bf16)
+    own = lax.dot_general(
+        pooling, full_ref[my_ref[0], 0], CONTRACT_LAST, preferred_element_type=f32
+    )
     attended = jnp.dot(pooled, wout_ref[...], preferred_element_type=f32)
     for part in range(parts):
         block = attended[:, part * part_width : (part + 1) * part_width]
         out_ref[part, 0] = (block + jnp.where(my_ref[0] == part, own, 0.0)).astype(bf16)
 
 
-def attend(full, own, valid_count, my, ln_gain, w_qkv, w_out):
-    parts, frames, patch_count, part_width = full.shape
+def attend(full, valid_count, my, gain, w_qkv, w_out):
+    parts, frames, part_width, patch_count = full.shape
     width = parts * part_width
-    local_width = w_qkv.shape[2]
+    local_width = w_qkv.shape[1]
     tokens = patch_count // POOL
     return pl.pallas_call(
         attend_kernel,
@@ -83,30 +91,39 @@
             num_scalar_prefetch=2,
             grid=(frames,),
             in_specs=[
-                pl.BlockSpec((parts, 1, patch_count, part_width), lambda f, *_: (0, f, 0, 0)),
-                pl.BlockSpec((1, patch_count, part_width), lambda f, *_: (f, 0, 0)),
-                pl.BlockSpec((parts, 1, part_width), lambda f, *_: (0, 0, 0)),
-                pl.BlockSpec((3, width, local_width), lambda f, *_: (0, 0, 0)),
+                pl.BlockSpec((parts, 1, part_width, patch_count), lambda f, *_: (0, f, 0, 0)),
+                pl.BlockSpec((parts, part_width, 1), lambda f, *_: (0, 0, 0)),
+                pl.BlockSpec((3, local_width, width), lambda f, *_: (0, 0, 0)),
                 pl.BlockSpec((local_width, width), lambda f, *_: (0, 0)),
             ],
             out_specs=pl.BlockSpec((parts, 1, tokens, part_width), lambda f, *_: (0, f, 0, 0)),
             scratch_shapes=[
-                VMEM((patch_count, width), bf16),
-                VMEM((patch_count, local_width), bf16),
+                VMEM((width, patch_count), bf16),
+                VMEM((local_width, patch_count), f32),
             ],
         ),
+        cost_estimate=pl.CostEstimate(
+            flops=frames * patch_count * width * local_width * 10,
+            bytes_accessed=12_000_000,
+            transcendentals=4_000_000,
+        ),
         name="attend",
-    )(valid_count, my, full, own, ln_gain.reshape(parts, 1, part_width), w_qkv, w_out)
-
-
-def bucket_kernel(slot_ref, label_ref, count_ref, parts_ref, out_ref):
-    parts, _, tokens, part_width = parts_ref.shape
+    )(valid_count, my, full, gain, w_qkv, w_out)
+
+
+def bucket_kernel(slot_ref, label_ref, count_ref, *refs):
+    pieces, out_ref = refs[:-1], refs[-1]
+    parts, size, tokens, part_width = pieces[0].shape
     padded = out_ref.shape[2]
     spot = lax.broadcasted_iota(jnp.int32, (tokens, part_width), 0) * POOL
 
     def step(target, carry):
         slot = slot_ref[target]
-        total = sum(parts_ref[part, slot].astype(f32) for part in range(parts))
+        total = jnp.zeros((tokens, part_width), f32)
+        for piece, ref in enumerate(pieces):
+            inside = jnp.clip(slot - piece * size, 0, size - 1)
+            here = sum(ref[part, inside].astype(f32) for part in range(parts))
+            total = jnp.where(slot // size == piece, here, total)
         kept = jnp.where(spot < count_ref[target], total, 0.0)
         out_ref[target, :, :part_width] = kept.astype(bf16)
         out_ref[target, :, part_width:] = jnp.full(
@@ -118,21 +135,23 @@
 
 
 def bucket(parts, frame_ids, valid_count, shards):
-    frames, tokens, part_width = parts.shape[1:]
+    tokens, part_width = parts[0].shape[2:]
+    frames = frame_ids.shape[0]
     padded = (part_width // LANES + 1) * LANES
     onehot = (frame_ids // frames)[None, :] == jnp.arange(shards)[:, None]
     pick = lambda row: jnp.sum(jnp.where(onehot, row[None, :], 0), axis=1).astype(jnp.int32)
     return pl.pallas_call(
         bucket_kernel,
         out_shape=jax.ShapeDtypeStruct((shards, tokens, padded), bf16),
-        in_specs=[pl.BlockSpec(memory_space=pltpu.SMEM)] * 3 + [pl.BlockSpec(memory_space=VMEM)],
+        in_specs=[pl.BlockSpec(memory_space=pltpu.SMEM)] * 3
+        + [pl.BlockSpec(memory_space=VMEM)] * len(parts),
         out_specs=pl.BlockSpec(memory_space=VMEM),
         name="bucket",
     )(
         pick(jnp.arange(frames, dtype=jnp.int32)),
         pick(frame_ids % frames + 1),
         pick(valid_count),
-        parts,
+        *parts,
     )
 
 
@@ -233,7 +252,7 @@
 
 
 def local_kernel(
-    inner_ref, write_ref, read_ref, down_ref, across_ref, step_ref, left_ref, skip_ref, out_ref, state
+    inner_ref, write_ref, read_ref, down_ref, across_ref, step_ref, skip_ref, out_ref, state
 ):
     length, features = inner_ref.shape
 
@@ -247,29 +266,31 @@
         jnp.int32, (length, length), 1
     )
     crossing = jnp.where(causal, crossing, 0.0)
-    down, across, steps, left = down_ref[0], across_ref[0], step_ref[0], left_ref[0]
-    grown = jnp.exp(down)
+    down, across, steps = down_ref[0], across_ref[0], step_ref[0]
+    grown = jnp.exp2(down)
+    left = jnp.exp2(down[length - 1 :, :] - down)
     lane = lax.broadcasted_iota(jnp.int32, (length, LANES), 1)
     row = lax.broadcasted_iota(jnp.int32, (LANES, STATE), 0)
     for pair in range(features // LANES):
         at = slice(pair * LANES, (pair + 1) * LANES)
-        inner = inner_ref[:, at]
+        inner = inner_ref[:, at].astype(f32)
+        weighted = inner * paired(steps, pair, length)
+        stepped = weighted.astype(bf16)
         halves = []
         for head in (2 * pair, 2 * pair + 1):
             spans = jnp.minimum(down[:, head : head + 1] - across[head : head + 1, :], 0.0)
-            mixing = crossing * jnp.exp(spans) * steps[head : head + 1, :]
-            halves.append(jnp.dot(mixing.astype(bf16), inner, preferred_element_type=f32))
+            mixing = crossing * jnp.exp2(spans)
+            halves.append(jnp.dot(mixing.astype(bf16), stepped, preferred_element_type=f32))
         held = state[at, :]
         carried = lax.dot_general(
             readers, held.astype(bf16), CONTRACT_LAST, preferred_element_type=f32
         )
-        inner = inner.astype(f32)
         out_ref[:, at] = (
             jnp.where(lane < HDIM, halves[0], halves[1])
             + carried * paired(grown, pair, length)
             + skip_ref[:, at] * inner
         )
-        scaled = (inner * paired(left, pair, length)).astype(bf16)
+        scaled = (weighted * paired(left, pair, length)).astype(bf16)
         last = grown[length - 1 :, :]
         faded = held * jnp.where(
             row < HDIM, last[:, 2 * pair : 2 * pair + 1], last[:, 2 * pair + 1 : 2 * pair + 2]
@@ -279,7 +300,7 @@
         )
 
 
-def local_outputs(inner, write, read, down, across, steps, left, skip):
+def local_outputs(inner, write, read, down, across, steps, skip):
     length = inner.shape[0]
     groups, _, per_group = down.shape
     features = inner.shape[1] // groups
@@ -295,7 +316,6 @@
             pl.BlockSpec((CHUNK, STATE), lambda g, c: (c, g)),
             tall,
             flat,
-            flat,
             tall,
             pl.BlockSpec((1, features), lambda g, c: (0, g)),
         ],
@@ -305,7 +325,7 @@
             flops=20_000_000_000, bytes_accessed=20_000_000, transcendentals=4_000_000
         ),
         name="local_outputs",
-    )(inner, write, read, down, across, steps, left, skip)
+    )(inner, write, read, down, across, steps, skip)
 
 
 def prefix_kernel(arrived_ref, decay_ref, out_ref):
@@ -400,11 +420,26 @@
     frame_count, patch_count, part_width = patches.shape
     shards = lax.axis_size("tm")
     my = lax.axis_index("head").astype(jnp.int32).reshape(1)
-    full = lax.all_gather(patches, "head")
+    sideways = patches.swapaxes(1, 2)
+    pieces = 2 if frame_count % 2 == 0 else 1
+    size = frame_count // pieces
+    cuts = [slice(piece * size, (piece + 1) * size) for piece in range(pieces)]
+    gathered = [lax.all_gather(sideways[cut], "head") for cut in cuts]
     all_conn = lax.all_gather(w_conn, "head")
     valid_count = (grid_rows * GRID).astype(jnp.int32)
-    parts = attend(full, patches, valid_count, my, ln_gain, w_qkv, w_out)
-    parts = lax.all_to_all(parts, "head", split_axis=0, concat_axis=0, tiled=True)
+    gain = ln_gain.reshape(-1, part_width, 1)
+    w_across = w_qkv.swapaxes(1, 2)
+    parts = [
+        lax.all_to_all(
+            attend(full, valid_count[cut], my, gain, w_across, w_out),
+            "head",
+            split_axis=0,
+            concat_axis=0,
+            tiled=True,
+        )
+        for cut, full in zip(cuts, gathered)
+    ]
+    parts, all_conn = lax.optimization_barrier((parts, all_conn))
     outgoing = bucket(parts, frame_ids, valid_count, shards)
     incoming = lax.all_to_all(outgoing, "tm", split_axis=0, concat_axis=0, tiled=True)
     labels = incoming[:, 0, part_width].astype(jnp.int32)
@@ -439,15 +474,14 @@
     flat = lambda member: member.reshape(tokens, groups, per_group).transpose(1, 2, 0)
     state = final_state(inner, write, tall(step_size * jnp.exp(total_log - from_start)))
     before = incoming_state(state, jnp.repeat(total_log, HDIM), shards)
-    left = step_size * jnp.exp(ends[:, None, :] - cumul).reshape(tokens, heads)
+    doubling = cumul * math.log2(math.e)
     local = local_outputs(
         inner,
         write,
         read,
-        tall(cumul),
-        flat(cumul),
-        flat(step_size),
-        tall(left),
+        tall(doubling),
+        flat(doubling),
+        tall(step_size),
         jnp.repeat(d_skip, HDIM).reshape(1, -1),
     )
     return stream_rows, finish(local, read, before, tall(jnp.exp(from_start)), out_gain)

time: 304 us -> 297 us (0.977)
  local copies, waits for them, and re-layouts: 34.8 us -> 16.5 us
  Pallas kernels: 131 us -> 136 us
  starting transfers between devices: 11.2 us -> 15.4 us
  waiting for transfers between devices: 18.6 us -> 22.4 us
    unnamed x39 -> x35, local copies, waits for them, and re-layouts: 13.7 us -> 0.88 us
    all_gather x1 -> x0, local copies, waits for them, and re-layouts: 10.7 us -> none  [on_device(): full = lax.all_gather(patches, 'head')]
    slice x0 -> x2, local copies, waits for them, and re-layouts: none -> 4.65 us  [the longest x1 4.06 us: on_device(): gathered = [lax.all_gather(sideways[cut], 'head') for cut in cuts]]
    all_gather x1 -> x2, waiting for transfers between devices: 7.45 us -> 11.5 us  [on_device(): gathered = [lax.all_gather(sideways[cut], 'head') for cut in cuts]]
    all_to_all x0 -> x1, starting transfers between devices: none -> 3.72 us  [on_device(): lax.all_to_all(attend(full, valid_count[cut], my, gain, w_across, w_out),...]
    pallas_call x1 -> x2, Pallas kernels: 60 us -> 62.7 us  [attend(): pl.pallas_call(attend_kernel, out_shape=jax.ShapeDtypeStruct((parts, fram...]
  transfers between devices with their start and end apart: 5 -> 7, of which waited for: 3 -> 3; matrix products, arithmetic and copies ran while one was open for 14% -> 6% of each run, Pallas kernels for 29% -> 30%
where the time goes in v2:
time: 297 us; the launch traced here: 295 us
  Pallas kernels  136 us (46%)
  blocking collectives  46.3 us (16%)
  matrix products  39.3 us (13%)
  waiting for transfers between devices  22.4 us (8%)
  local copies, waits for them, and re-layouts  16.5 us (6%)
  starting transfers between devices  15.4 us (5%)
  between operations  14 us (5%)
  other arithmetic  5.25 us (2%)
    pallas_call x2, Pallas kernels, attend(): pl.pallas_call(attend_kernel, out_shape=jax.ShapeDtypeStruct((parts, fram...  62.7 us
    all_to_all x1, blocking collectives, on_device(): lax.all_to_all(outgoing, 'tm', split_axis=0, concat_axis=0, tiled=True)  39.7 us
    pallas_call x1, Pallas kernels, local_outputs(): pl.pallas_call(local_kernel, out_shape=jax.ShapeDtypeStruct(inner.shape,...  27.2 us
    dot_general x1, matrix products, on_device(): inner = jnp.dot(normed, w_x, preferred_element_type=f32).astype(bf16)  21.8 us
    pallas_call x1, Pallas kernels, connect(): pl.pallas_call(connect_kernel, out_shape=(jax.ShapeDtypeStruct((frames *...  19.1 us
    pallas_call x1, Pallas kernels, finish(): pl.pallas_call(finish_kernel, out_shape=jax.ShapeDtypeStruct(local.shape,...  13.3 us
    all_gather x2, waiting for transfers between devices, on_device(): gathered = [lax.all_gather(sideways[cut], 'head') for cut in cuts]  11.5 us
    dot_general x1, matrix products, on_device(): read = jnp.dot(normed, w_c, preferred_element_type=f32).astype(bf16)  8.29 us
  transfers between devices with their start and end apart: 7, of which 3 were waited for; matrix products, arithmetic and copies ran while one was open for 6% of the time, Pallas kernels for 30%

profile of v2, /device:TPU:0, one launch (start us, length us, event | category | flops | bytes accessed | tf_op | source)
XLA Modules:
  0.0 295.0 jit_solution(9181687429774689229)
XLA Ops:
  7.2 0.0 copy-start
  7.2 0.0 all-gather.9.cloned.1.call-start
  7.2 4.1 %fusion.5 = (bf16[6,576,256]{2,1,0:T(8,128)(2,1)}, bf16[6,576,256]{2,1,0:T(8,128)(2,1)}) fusion(bf16[12,576,256]{2,1,0:T(8,128)(2,1)} %bitcast.48), kind=kLoop, calls=%fused_computation.34 | loop fusion | bytes 7077888 | tf_op jit(solution)/shard_map/slice | solution.py:427
  11.3 0.0 all-gather.9.cloned.1.call-update
  11.3 0.0 all-gather.11.cloned.1.call-start
  11.4 0.7 all-gather.11.cloned.1.call-update
  12.1 0.0 all-gather.13.cloned.1.call-start
  12.1 0.7 all-gather.13.cloned.1.call-update
  12.8 0.0 copy-done.6
  12.8 1.3 reshape.121.gain_ref
  14.1 0.0 copy-done.8
  14.1 0.7 select_reduce_fusion.1
  14.8 0.6 fusion.6
  15.4 11.5 %all-gather.9.cloned.1.call-done = bf16[12,576,256]{2,1,0:T(8,128)(2,1)} async-done(((bf16[6,576,256]{2,1,0:T(8,128)(2,1)}), bf16[12,576,256]{2,1,0:T(8,128)(2,1)}) %all-gather.9.cloned.1.call-update) | async-done | bytes 3538960 | tf_op jit(solution)/shard_map/all_gather | solution.py:427
  26.9 31.3 %attend.2 = bf16[2,6,64,576]{3,2,1,0:T(8,128)(2,1)} custom-call(s32[6]{0:T(128)} %get-tuple-element.23.valid_ref, s32[1]{0:T(128)} %bitcast.my_ref, bf16[2,6,576,256]{3,2,1,0:T(8,128)(2,1)} %bitcast.67, f32[2,576,1]{2,1,0:T(8,128)} %reshape.121.gain_ref, bf16[3,576,1152]{2,1,0:T(8,128)(2,1)} %bitcast.64, bf16[576,1152]{1,0:T(8,128)(2,1)} %wout_ref.3), custom_call_target="tpu_custom_call" | custom-call | flops 10192158720 | bytes 12000000 | tf_op jit(solution)/shard_map/attend/pallas_call | solution.py:87
  58.2 3.7 %all-to-all-start = ((bf16[2,6,64,576]{3,2,1,0:T(8,128)(2,1)}), bf16[2,6,64,576]{3,2,1,0:T(8,128)(2,1)S(1)}, u32[]{:S(2)}, u32[]{:S(2)}) async-start(bf16[2,6,64,576]{3,2,1,0:T(8,128)(2,1)} %attend.2), calls=%async_computation | async-start | bytes 1966080 | tf_op jit(solution)/shard_map/all_to_all | solution.py:433
  62.0 0.0 all-gather.15.cloned.1.call-start
  62.0 0.0 all-gather.11.cloned.1.call-done
  62.0 31.3 %attend.3 = bf16[2,6,64,576]{3,2,1,0:T(8,128)(2,1)} custom-call(s32[6]{0:T(128)} %get-tuple-element.22.valid_ref, s32[1]{0:T(128)} %bitcast.my_ref, bf16[2,6,576,256]{3,2,1,0:T(8,128)(2,1)} %bitcast.66, f32[2,576,1]{2,1,0:T(8,128)} %reshape.121.gain_ref, bf16[3,576,1152]{2,1,0:T(8,128)(2,1)} %bitcast.65, bf16[576,1152]{1,0:T(8,128)(2,1)} %wout_ref.3), custom_call_target="tpu_custom_call" | custom-call | flops 10192158720 | bytes 12000000 | tf_op jit(solution)/shard_map/attend/pallas_call | solution.py:87
  93.4 0.0 all-to-all-done.refs_0_
  93.4 6.5 %all_to_all.25.refs_1_ = bf16[2,6,64,576]{3,2,1,0:T(8,128)(2,1)} all-to-all(bf16[2,6,64,576]{3,2,1,0:T(8,128)(2,1)} %attend.3), channel_id=1, replica_groups=mesh['tm'=16,'head'=2] {'head'}, dimensions={0} | all-to-all | bytes 1769472 | tf_op jit(solution)/shard_map/all_to_all | solution.py:433
  99.9 3.6 %bucket.1 = bf16[16,64,640]{2,1,0:T(8,128)(2,1)} custom-call(s32[16]{0:T(128)} %get-tuple-element.14.slot_ref, s32[16]{0:T(128)} %get-tuple-element.13.label_ref, s32[16]{0:T(128)} %get-tuple-element.12.count_ref, bf16[2,6,64,576]{3,2,1,0:T(8,128)(2,1)} %copy-done.2, bf16[2,6,64,576]{3,2,1,0:T(8,128)(2,1)} %all_to_all.25.refs_1_), custom_call_target="tpu_custom_call" | custom-call | tf_op jit(solution)/shard_map/bucket/pallas_call | solution.py:143
  103.5 39.7 %all_to_all.26 = bf16[16,64,640]{2,1,0:T(8,128)(2,1)} all-to-all(bf16[16,64,640]{2,1,0:T(8,128)(2,1)} %bucket.1), channel_id=1, replica_groups=mesh['tm'=16,'head'=2] {'tm'}, dimensions={0} | all-to-all | bytes 2621440 | tf_op jit(solution)/shard_map/all_to_all | solution.py:444
  143.2 0.0 all-gather.15.cloned.1.call-update
  143.3 1.2 fusion.1
  144.5 0.7 select_reduce_fusion.sender_ref
  145.2 7.3 %all-gather.15.cloned.1.call-done = bf16[32,64,640]{2,1,0:T(8,128)(2,1)} async-done(((bf16[16,64,640]{2,1,0:T(8,128)(2,1)}), bf16[32,64,640]{2,1,0:T(8,128)(2,1)}) %all-gather.15.cloned.1.call-update) | async-done | bytes 2621456 | tf_op jit(solution)/shard_map/all_gather | solution.py:454
  152.5 19.1 %connect.1 = (bf16[768,2048]{1,0:T(8,128)(2,1)}, bf16[768,4096]{1,0:T(8,128)(2,1)}) custom-call(s32[12]{0:T(128)} %select_reduce_fusion.sender_ref, s32[1]{0:T(128)} %bitcast.my_ref, bf16[2,16,64,640]{3,2,1,0:T(8,128)(2,1)} %bitcast.49, bf16[2,1152,2048]{2,1,0:T(8,128)(2,1)} %bitcast.43, f32[1,4096]{1,0:T(1,128)} %bitcast.61), custom_call_target="tpu_custom_call" | custom-call | tf_op jit(solution)/shard_map/connect/pallas_call | solution.py:191
  171.7 0.0 copy-done
  171.7 4.8 %broadcast_multiply_fusion.1 = (f32[768,32]{0,1:T(8,128)S(1)}, f32[768,32]{0,1:T(8,128)S(1)}) fusion(f32[32]{0:T(128)S(1)} %exponential_negate_fusion, f32[32]{0:T(128)S(1)} %copy-done.7, bf16[768,4096]{1,0:T(8,128)(2,1)} %get-tuple-element.11, bf16[4096,32]{0,1:T(8,128)(2,1)S(1)} %copy-done), kind=kOutput, calls=%fused_computation.11 | convolution fusion | flops 201523200 | bytes 6750464 | tf_op jit(solution)/shard_map/dot_general | solution.py:462
  176.5 0.2 copy.55
  176.6 0.4 reduce_window_sum.22
  177.0 0.1 fusion.4
  177.1 0.1 copy.56
  177.3 0.1 broadcast_in_dim.66
  177.4 0.1 multiply_bitcast_fusion
  177.5 0.0 slice-start
  177.5 1.7 copy.51
  179.1 21.8 %convolution_convert_fusion.inner_ref = bf16[768,2048]{1,0:T(8,128)(2,1)} fusion(bf16[768,4096]{1,0:T(8,128)(2,1)} %get-tuple-element.11, bf16[4096,2048]{1,0:T(8,128)(2,1)} %param.24), kind=kOutput, calls=%fused_computation | convolution fusion | flops 12886474752 | bytes 26214400 | tf_op jit(solution)/shard_map/dot_general | solution.py:464
  201.0 4.3 %convolution_convert_fusion.2.write_ref = bf16[768,512]{1,0:T(8,128)(2,1)} fusion(bf16[768,4096]{1,0:T(8,128)(2,1)S(1)} %bitcast.45, bf16[4096,512]{1,0:T(8,128)(2,1)S(1)} %copy-done.11), kind=kOutput, calls=%fused_computation.2 | convolution fusion | flops 3221618688 | bytes 11272192 | tf_op jit(solution)/shard_map/dot_general | solution.py:465
  205.4 0.1 broadcast_in_dim.67
  205.4 0.1 broadcast_in_dim.68
  205.6 0.0 copy-start.10
  205.6 7.4 %final_state.1 = bf16[2048,128]{1,0:T(8,128)(2,1)} custom-call(bf16[768,2048]{1,0:T(8,128)(2,1)} %convolution_convert_fusion.inner_ref, bf16[768,512]{1,0:T(8,128)(2,1)} %convolution_convert_fusion.2.write_ref, f32[4,768,8]{2,1,0:T(8,128)} %bitcast.46), custom_call_target="tpu_custom_call" | custom-call | tf_op jit(solution)/shard_map/final_state/pallas_call | solution.py:240
  213.0 1.9 pad_maximum_fusion
  214.9 6.8 %all-to-all-start.3 = ((bf16[16,144,128]{2,1,0:T(8,128)(2,1)}), bf16[16,144,128]{2,1,0:T(8,128)(2,1)S(1)}, u32[]{:S(2)}, u32[]{:S(2)}) async-start(bf16[16,144,128]{2,1,0:T(8,128)(2,1)} %pad_maximum_fusion), calls=%async_computation.3 | async-start | bytes 1179648 | tf_op jit(solution)/shard_map/all_to_all | solution.py:349
  221.7 0.1 broadcast_in_dim.65
  221.8 0.7 reshape_reshape.4.skip_ref
  222.4 0.2 copy.47
  222.7 1.6 copy.48
  224.3 1.7 copy.49
  226.0 0.2 copy.53
  226.2 1.7 copy.54
  227.8 8.3 %convolution_convert_fusion.1.read_ref = bf16[768,512]{1,0:T(8,128)(2,1)} fusion(bf16[768,4096]{1,0:T(8,128)(2,1)} %get-tuple-element.11, bf16[4096,512]{1,0:T(8,128)(2,1)} %param.26), kind=kOutput, calls=%fused_computation.1 | convolution fusion | flops 3221618688 | bytes 11272192 | tf_op jit(solution)/shard_map/dot_general | solution.py:466
  236.1 2.2 all-to-all-done.3.arrived_ref
  238.3 0.1 reshape.116
  238.4 1.3 copy.52.decay_ref
  239.8 2.6 prefix.1
  242.3 4.7 %all-to-all-start.4 = ((bf16[16,128,128]{2,1,0:T(8,128)(2,1)}), bf16[16,128,128]{2,1,0:T(8,128)(2,1)S(1)}, u32[]{:S(2)}, u32[]{:S(2)}) async-start(bf16[16,128,128]{2,1,0:T(8,128)(2,1)} %prefix.1), calls=%async_computation.4 | async-start | bytes 1048576 | tf_op jit(solution)/shard_map/all_to_all | solution.py:359
  247.1 27.2 %local_outputs.1.local_ref = f32[768,2048]{1,0:T(8,128)} custom-call(bf16[768,2048]{1,0:T(8,128)(2,1)} %convolution_convert_fusion.inner_ref, bf16[768,512]{1,0:T(8,128)(2,1)} %convolution_convert_fusion.2.write_ref, bf16[768,512]{1,0:T(8,128)(2,1)} %convolution_convert_fusion.1.read_ref, f32[4,768,8]{2,1,0:T(8,128)} %bitcast.52, f32[4,8,768]{2,1,0:T(8,128)} %bitcast.57, ...), custom_call_target="tpu_custom_call" | custom-call | flops 20000000000 | bytes 20000000 | tf_op jit(solution)/shard_map/local_outputs/pallas_call | solution.py:309
  274.3 0.0 all-to-all-done.4
  274.3 0.0 copy-start.1
  274.4 0.8 copy-done.4
  275.1 13.3 %finish.1 = bf16[768,2048]{1,0:T(8,128)(2,1)} custom-call(f32[768,2048]{1,0:T(8,128)} %local_outputs.1.local_ref, bf16[768,512]{1,0:T(8,128)(2,1)} %convolution_convert_fusion.1.read_ref, bf16[2048,128]{1,0:T(8,128)(2,1)} %bitcast.51, f32[4,768,8]{2,1,0:T(8,128)} %bitcast.47, f32[1,2048]{1,0:T(1,128)} %bitcast.63), custom_call_target="tpu_custom_call" | custom-call | tf_op jit(solution)/shard_map/finish/pallas_call | solution.py:385
  (39 shorter events, 0.2 us)
Async XLA Ops:
  7.2 164.5 %copy-start = (bf16[4096,32]{0,1:T(8,128)(2,1)S(1)}, bf16[4096,32]{0,1:T(8,128)(2,1)}, u32[]{:S(2)}) copy-start(bf16[4096,32]{0,1:T(8,128)(2,1)} %param.27) | copy-start | bytes 786436
  7.2 19.7 %all-gather.9.cloned.1.call-start = ((), (), s32[]{:S(2)}) async-start(), calls=%async_computation.5 | async-start | bytes 5308416 | tf_op jit(solution)/shard_map/all_gather | solution.py:427
  11.3 1.5 copy-start.6
  11.3 2.8 copy-start.8
  11.3 2.8 copy-start.9
  11.3 50.7 %all-gather.11.cloned.1.call-start = ((), (), s32[]{:S(2)}) async-start(), calls=%async_computation.6 | async-start | bytes 5308416 | tf_op jit(solution)/shard_map/all_gather | solution.py:427
  12.1 87.9 %all-gather.13.cloned.1.call-start = ((), (), s32[]{:S(2)}) async-start(), calls=%async_computation.7 | async-start | bytes 14155776 | tf_op jit(solution)/shard_map/all_gather | solution.py:428
  58.2 35.1 %all-to-all-start = ((bf16[2,6,64,576]{3,2,1,0:T(8,128)(2,1)}), bf16[2,6,64,576]{3,2,1,0:T(8,128)(2,1)S(1)}, u32[]{:S(2)}, u32[]{:S(2)}) async-start(bf16[2,6,64,576]{3,2,1,0:T(8,128)(2,1)} %attend.2), calls=%async_computation | async-start | bytes 1966080 | tf_op jit(solution)/shard_map/all_to_all | solution.py:433
  62.0 90.6 %all-gather.15.cloned.1.call-start = ((), (), s32[]{:S(2)}) async-start(), calls=%async_computation.8 | async-start | bytes 3932160 | tf_op jit(solution)/shard_map/all_gather | solution.py:454
  93.4 49.9 %copy-start.12 = (f32[32]{0:T(128)S(1)}, f32[32]{0:T(128)}, u32[]{:S(2)}) copy-start(f32[32]{0:T(128)} %param.29) | copy-start | bytes 388
  93.4 6.6 %copy-start.2 = (bf16[2,6,64,576]{3,2,1,0:T(8,128)(2,1)}, bf16[2,6,64,576]{3,2,1,0:T(8,128)(2,1)S(1)}, u32[]{:S(2)}) copy-start(bf16[2,6,64,576]{3,2,1,0:T(8,128)(2,1)S(1)} %all-to-all-done.refs_0_) | copy-start | bytes 2654212
  152.5 19.1 %copy-start.7 = (f32[32]{0:T(128)S(1)}, f32[32]{0:T(128)}, u32[]{:S(2)}) copy-start(f32[32]{0:T(128)} %param.28) | copy-start | bytes 388
  177.5 23.5 %slice-start = ((s8[6291456]{0:T(1024)(128)(4,1)}), s8[2097152]{0:T(1024)(128)(4,1)S(1)}, s32[]{:S(2)}) async-start(s8[6291456]{0:T(1024)(128)(4,1)} %bitcast.44), calls=%async_computation.9 | async-start | bytes 4194304
  179.1 21.9 %slice-start.1 = ((s8[6291456]{0:T(1024)(128)(4,1)}), s8[4194304]{0:T(1024)(128)(4,1)S(1)}, s32[]{:S(2)}) async-start(s8[6291456]{0:T(1024)(128)(4,1)} %bitcast.44), calls=%async_computation.10 | async-start | bytes 8388608
  179.1 21.9 %copy-start.11 = (bf16[4096,512]{1,0:T(8,128)(2,1)S(1)}, bf16[4096,512]{1,0:T(8,128)(2,1)}, u32[]{:S(2)}) copy-start(bf16[4096,512]{1,0:T(8,128)(2,1)} %param.25) | copy-start | bytes 12582916
  205.6 16.1 %copy-start.10 = (f32[32]{0:T(128)S(1)}, f32[32]{0:T(128)}, u32[]{:S(2)}) copy-start(f32[32]{0:T(128)} %param.30) | copy-start | bytes 388
  214.9 23.4 %all-to-all-start.3 = ((bf16[16,144,128]{2,1,0:T(8,128)(2,1)}), bf16[16,144,128]{2,1,0:T(8,128)(2,1)S(1)}, u32[]{:S(2)}, u32[]{:S(2)}) async-start(bf16[16,144,128]{2,1,0:T(8,128)(2,1)} %pad_maximum_fusion), calls=%async_computation.3 | async-start | bytes 1179648 | tf_op jit(solution)/shard_map/all_to_all | solution.py:349
  222.7 13.5 %copy-start.5 = (f32[768,4,8]{0,2,1:T(8,128)}, f32[768,4,8]{0,2,1:T(8,128)S(1)}, u32[]{:S(2)}) copy-start(f32[768,4,8]{0,2,1:T(8,128)S(1)} %mul.29) | copy-start | bytes 294916
  238.3 1.5 copy-start.3
  242.3 32.0 %all-to-all-start.4 = ((bf16[16,128,128]{2,1,0:T(8,128)(2,1)}), bf16[16,128,128]{2,1,0:T(8,128)(2,1)S(1)}, u32[]{:S(2)}, u32[]{:S(2)}) async-start(bf16[16,128,128]{2,1,0:T(8,128)(2,1)} %prefix.1), calls=%async_computation.4 | async-start | bytes 1048576 | tf_op jit(solution)/shard_map/all_to_all | solution.py:359
  274.3 0.8 copy-start.4
  274.3 14.1 %copy-start.1 = (bf16[4096,32]{0,1:T(8,128)(2,1)S(1)}, bf16[4096,32]{0,1:T(8,128)(2,1)}, u32[]{:S(2)}) copy-start(bf16[4096,32]{0,1:T(8,128)(2,1)} %param.27) | copy-start | bytes 786436
Sparse Core Ops, SparseCore 0:
  11.4 15.4 all-gather.8
  29.0 13.8 all-gather.10
  44.5 23.4 all-gather.12
  143.4 9.1 all-gather.14

commit v3 on v2

--- a/solution.py
+++ b/solution.py
@@ -63,7 +63,7 @@
         mixed = jnp.dot(
             values[at].astype(bf16), powered.astype(bf16), preferred_element_type=f32
         )
-        context[at, :] = mixed / total
+        context[at, :] = mixed * (1.0 / total)
     row = lax.broadcasted_iota(jnp.int32, (tokens, patch_count), 0)
     column = lax.broadcasted_iota(jnp.int32, (tokens, patch_count), 1)
     pooling = jnp.where(column // POOL == row, 1.0 / POOL, 0.0).astype(bf16)
@@ -113,17 +113,19 @@
 
 def bucket_kernel(slot_ref, label_ref, count_ref, *refs):
     pieces, out_ref = refs[:-1], refs[-1]
-    parts, size, tokens, part_width = pieces[0].shape
+    parts, _, tokens, part_width = pieces[0].shape
     padded = out_ref.shape[2]
     spot = lax.broadcasted_iota(jnp.int32, (tokens, part_width), 0) * POOL
 
     def step(target, carry):
         slot = slot_ref[target]
         total = jnp.zeros((tokens, part_width), f32)
-        for piece, ref in enumerate(pieces):
-            inside = jnp.clip(slot - piece * size, 0, size - 1)
+        start = 0
+        for ref in pieces:
+            inside = jnp.clip(slot - start, 0, ref.shape[1] - 1)
             here = sum(ref[part, inside].astype(f32) for part in range(parts))
-            total = jnp.where(slot // size == piece, here, total)
+            total = jnp.where(slot >= start, here, total)
+            start += ref.shape[1]
         kept = jnp.where(spot < count_ref[target], total, 0.0)
         out_ref[target, :, :part_width] = kept.astype(bf16)
         out_ref[target, :, part_width:] = jnp.full(
@@ -222,15 +224,16 @@
     )
 
 
-def final_state_kernel(inner_ref, write_ref, weight_ref, out_ref):
+def final_state_kernel(inner_ref, write_ref, weight_ref, out_ref, scaled):
     length, features = inner_ref.shape
     weights = weight_ref[0]
     for pair in range(features // LANES):
         at = slice(pair * LANES, (pair + 1) * LANES)
-        scaled = (inner_ref[:, at].astype(f32) * paired(weights, pair, length)).astype(bf16)
-        out_ref[at, :] = lax.dot_general(
-            scaled, write_ref[...], CONTRACT_FIRST, preferred_element_type=f32
-        ).astype(bf16)
+        scaled[:, at] = (inner_ref[:, at].astype(f32) * paired(weights, pair, length)).astype(bf16)
+    sideways = lax.dot_general(
+        write_ref[...], scaled[...], CONTRACT_FIRST, preferred_element_type=f32
+    )
+    out_ref[...] = sideways.T.astype(bf16)
 
 
 def final_state(inner, write, weights):
@@ -247,12 +250,13 @@
             pl.BlockSpec((1, length, weights.shape[2]), lambda g: (g, 0, 0)),
         ],
         out_specs=pl.BlockSpec((features, STATE), lambda g: (g, 0)),
+        scratch_shapes=[VMEM((length, features), bf16)],
         name="final_state",
     )(inner, write, weights)
 
 
 def local_kernel(
-    inner_ref, write_ref, read_ref, down_ref, across_ref, step_ref, skip_ref, out_ref, state
+    inner_ref, write_ref, read_ref, down_ref, across_ref, step_ref, skip_ref, out_ref, state, scaled
 ):
     length, features = inner_ref.shape
 
@@ -270,34 +274,29 @@
     grown = jnp.exp2(down)
     left = jnp.exp2(down[length - 1 :, :] - down)
     lane = lax.broadcasted_iota(jnp.int32, (length, LANES), 1)
-    row = lax.broadcasted_iota(jnp.int32, (LANES, STATE), 0)
+    held = state[...]
+    carried = jnp.dot(readers, held.astype(bf16), preferred_element_type=f32)
     for pair in range(features // LANES):
         at = slice(pair * LANES, (pair + 1) * LANES)
         inner = inner_ref[:, at].astype(f32)
         weighted = inner * paired(steps, pair, length)
-        stepped = weighted.astype(bf16)
         halves = []
         for head in (2 * pair, 2 * pair + 1):
             spans = jnp.minimum(down[:, head : head + 1] - across[head : head + 1, :], 0.0)
-            mixing = crossing * jnp.exp2(spans)
-            halves.append(jnp.dot(mixing.astype(bf16), stepped, preferred_element_type=f32))
-        held = state[at, :]
-        carried = lax.dot_general(
-            readers, held.astype(bf16), CONTRACT_LAST, preferred_element_type=f32
+            halves.append((crossing * jnp.exp2(spans)).astype(bf16))
+        stacked = jnp.concatenate(
+            [jnp.where(lane < HDIM, weighted, 0.0), jnp.where(lane < HDIM, 0.0, weighted)], axis=0
+        ).astype(bf16)
+        within = jnp.dot(
+            jnp.concatenate(halves, axis=1), stacked, preferred_element_type=f32
         )
-        out_ref[:, at] = (
-            jnp.where(lane < HDIM, halves[0], halves[1])
-            + carried * paired(grown, pair, length)
-            + skip_ref[:, at] * inner
-        )
-        scaled = (weighted * paired(left, pair, length)).astype(bf16)
-        last = grown[length - 1 :, :]
-        faded = held * jnp.where(
-            row < HDIM, last[:, 2 * pair : 2 * pair + 1], last[:, 2 * pair + 1 : 2 * pair + 2]
-        )
-        state[at, :] = faded + lax.dot_general(
-            scaled, writers, CONTRACT_FIRST, preferred_element_type=f32
-        )
+        faded = paired(grown, pair, length)
+        out_ref[:, at] = within + carried[:, at] * faded + skip_ref[:, at] * inner
+        scaled[:, at] = (weighted * paired(left, pair, length)).astype(bf16)
+        state[:, at] = held[:, at] * faded[length - 1 :, :]
+    state[...] += lax.dot_general(
+        writers, scaled[...], CONTRACT_FIRST, preferred_element_type=f32
+    )
 
 
 def local_outputs(inner, write, read, down, across, steps, skip):
@@ -320,7 +319,7 @@
             pl.BlockSpec((1, features), lambda g, c: (0, g)),
         ],
         out_specs=pl.BlockSpec((CHUNK, features), lambda g, c: (c, g)),
-        scratch_shapes=[VMEM((features, STATE), f32)],
+        scratch_shapes=[VMEM((STATE, features), f32), VMEM((CHUNK, features), bf16)],
         cost_estimate=pl.CostEstimate(
             flops=20_000_000_000, bytes_accessed=20_000_000, transcendentals=4_000_000
         ),
@@ -365,12 +364,12 @@
     length, features = local_ref.shape
     grown = grown_ref[0]
     squares = 0.0
+    carried = lax.dot_general(
+        read_ref[...], state_ref[...], CONTRACT_LAST, preferred_element_type=f32
+    )
     for pair in range(features // LANES):
         at = slice(pair * LANES, (pair + 1) * LANES)
-        carried = lax.dot_general(
-            read_ref[...], state_ref[at, :], CONTRACT_LAST, preferred_element_type=f32
-        )
-        summed = local_ref[:, at] + carried * paired(grown, pair, length)
+        summed = local_ref[:, at] + carried[:, at] * paired(grown, pair, length)
         total[:, at] = summed
         squares = squares + jnp.sum(summed * summed, axis=-1, keepdims=True)
     scale = lax.rsqrt(squares / features + 1e-05)
@@ -421,9 +420,8 @@
     shards = lax.axis_size("tm")
     my = lax.axis_index("head").astype(jnp.int32).reshape(1)
     sideways = patches.swapaxes(1, 2)
-    pieces = 2 if frame_count % 2 == 0 else 1
-    size = frame_count // pieces
-    cuts = [slice(piece * size, (piece + 1) * size) for piece in range(pieces)]
+    first = max(frame_count // 4, 1)
+    cuts = [cut for cut in (slice(0, first), slice(first, frame_count)) if cut.start < cut.stop]
     gathered = [lax.all_gather(sideways[cut], "head") for cut in cuts]
     all_conn = lax.all_gather(w_conn, "head")
     valid_count = (grid_rows * GRID).astype(jnp.int32)

time: 297 us -> 291 us (0.980)
  waiting for transfers between devices: 22.4 us -> 16.9 us
    all_gather x2, waiting for transfers between devices: 11.5 us -> 6.7 us  [on_device(): gathered = [lax.all_gather(sideways[cut], 'head') for cut in cuts]]
  transfers between devices with their start and end apart: 7 -> 7, of which waited for: 3 -> 3; matrix products, arithmetic and copies ran while one was open for 6% -> 8% of each run, Pallas kernels for 30% -> 30%
where the time goes in v3:
time: 291 us; the launch traced here: 289 us
  Pallas kernels  134 us (46%)
  blocking collectives  47.3 us (16%)
  matrix products  39.3 us (14%)
  local copies, waits for them, and re-layouts  18 us (6%)
  waiting for transfers between devices  16.9 us (6%)
  starting transfers between devices  15.2 us (5%)
  between operations  14 us (5%)
  other arithmetic  5.22 us (2%)
    pallas_call x2, Pallas kernels, attend(): pl.pallas_call(attend_kernel, out_shape=jax.ShapeDtypeStruct((parts, fram...  62.7 us
    all_to_all x1, blocking collectives, on_device(): lax.all_to_all(outgoing, 'tm', split_axis=0, concat_axis=0, tiled=True)  39.7 us
    pallas_call x1, Pallas kernels, local_outputs(): pl.pallas_call(local_kernel, out_shape=jax.ShapeDtypeStruct(inner.shape,...  24.6 us
    dot_general x1, matrix products, on_device(): inner = jnp.dot(normed, w_x, preferred_element_type=f32).astype(bf16)  21.8 us
    pallas_call x1, Pallas kernels, connect(): pl.pallas_call(connect_kernel, out_shape=(jax.ShapeDtypeStruct((frames *...  19.1 us
    pallas_call x1, Pallas kernels, finish(): pl.pallas_call(finish_kernel, out_shape=jax.ShapeDtypeStruct(local.shape,...  13.9 us
    dot_general x1, matrix products, on_device(): read = jnp.dot(normed, w_c, preferred_element_type=f32).astype(bf16)  8.29 us
    all_to_all x1, blocking collectives, on_device(): lax.all_to_all(attend(full, valid_count[cut], my, gain, w_across, w_out),...  7.56 us
  transfers between devices with their start and end apart: 7, of which 3 were waited for; matrix products, arithmetic and copies ran while one was open for 8% of the time, Pallas kernels for 30%

profile of v3, /device:TPU:0, one launch (start us, length us, event | category | flops | bytes accessed | tf_op | source)
XLA Modules:
  0.0 289.5 jit_solution(14489879964046287238)
XLA Ops:
  7.2 0.0 copy-start
  7.2 0.0 all-gather.9.cloned.1.call-start
  7.2 2.2 slice.39
  9.4 0.0 all-gather.9.cloned.1.call-update
  9.4 0.0 all-gather.11.cloned.1.call-start
  9.5 3.4 %slice.40 = bf16[9,576,256]{2,1,0:T(8,128)(2,1)} slice(bf16[12,576,256]{2,1,0:T(8,128)(2,1)} %bitcast.50), slice={[3:12], [0:576], [0:256]} | slice | bytes 5308416 | tf_op jit(solution)/shard_map/slice | solution.py:425
  12.9 0.0 all-gather.11.cloned.1.call-update
  12.9 0.0 all-gather.13.cloned.1.call-start
  13.0 0.7 all-gather.13.cloned.1.call-update
  13.7 0.6 slice.32.valid_ref
  14.3 1.3 reshape.121.gain_ref
  15.6 0.7 select_reduce_fusion.1
  16.3 6.7 %all-gather.9.cloned.1.call-done = bf16[6,576,256]{2,1,0:T(8,128)(2,1)} async-done(((bf16[3,576,256]{2,1,0:T(8,128)(2,1)}), bf16[6,576,256]{2,1,0:T(8,128)(2,1)}) %all-gather.9.cloned.1.call-update) | async-done | bytes 1769488 | tf_op jit(solution)/shard_map/all_gather | solution.py:425
  23.0 0.0 copy-done.9
  23.0 17.8 %attend.2 = bf16[2,3,64,576]{3,2,1,0:T(8,128)(2,1)} custom-call(s32[3]{0:T(128)} %bitcast.66, s32[1]{0:T(128)} %bitcast.my_ref, bf16[2,3,576,256]{3,2,1,0:T(8,128)(2,1)} %bitcast.70, f32[2,576,1]{2,1,0:T(8,128)} %reshape.121.gain_ref, bf16[3,576,1152]{2,1,0:T(8,128)(2,1)} %bitcast.68, bf16[576,1152]{1,0:T(8,128)(2,1)} %wout_ref.3), custom_call_target="tpu_custom_call" | custom-call | flops 5096079360 | bytes 12000000 | tf_op jit(solution)/shard_map/attend/pallas_call | solution.py:87
  40.7 3.5 %all-to-all-start = ((bf16[2,3,64,576]{3,2,1,0:T(8,128)(2,1)}), bf16[2,3,64,576]{3,2,1,0:T(8,128)(2,1)S(1)}, u32[]{:S(2)}, u32[]{:S(2)}) async-start(bf16[2,3,64,576]{3,2,1,0:T(8,128)(2,1)} %attend.2), calls=%async_computation | async-start | bytes 983040 | tf_op jit(solution)/shard_map/all_to_all | solution.py:431
  44.2 0.0 all-gather.15.cloned.1.call-start
  44.3 0.0 all-gather.11.cloned.1.call-done
  44.3 44.9 %attend.3 = bf16[2,9,64,576]{3,2,1,0:T(8,128)(2,1)} custom-call(s32[9]{0:T(128)} %slice.32.valid_ref, s32[1]{0:T(128)} %bitcast.my_ref, bf16[2,9,576,256]{3,2,1,0:T(8,128)(2,1)} %bitcast.67, f32[2,576,1]{2,1,0:T(8,128)} %reshape.121.gain_ref, bf16[3,576,1152]{2,1,0:T(8,128)(2,1)} %bitcast.69, bf16[576,1152]{1,0:T(8,128)(2,1)} %wout_ref.3), custom_call_target="tpu_custom_call" | custom-call | flops 15288238080 | bytes 12000000 | tf_op jit(solution)/shard_map/attend/pallas_call | solution.py:87
  89.2 0.0 all-to-all-done.refs_0_
  89.2 7.6 %all_to_all.25.refs_1_ = bf16[2,9,64,576]{3,2,1,0:T(8,128)(2,1)} all-to-all(bf16[2,9,64,576]{3,2,1,0:T(8,128)(2,1)} %attend.3), channel_id=1, replica_groups=mesh['tm'=16,'head'=2] {'head'}, dimensions={0} | all-to-all | bytes 2654208 | tf_op jit(solution)/shard_map/all_to_all | solution.py:431
  96.8 3.6 %bucket.1 = bf16[16,64,640]{2,1,0:T(8,128)(2,1)} custom-call(s32[16]{0:T(128)} %get-tuple-element.14.slot_ref, s32[16]{0:T(128)} %get-tuple-element.13.label_ref, s32[16]{0:T(128)} %get-tuple-element.12.count_ref, bf16[2,3,64,576]{3,2,1,0:T(8,128)(2,1)} %copy-done.4, bf16[2,9,64,576]{3,2,1,0:T(8,128)(2,1)} %all_to_all.25.refs_1_), custom_call_target="tpu_custom_call" | custom-call | tf_op jit(solution)/shard_map/bucket/pallas_call | solution.py:145
  100.4 39.7 %all_to_all.26 = bf16[16,64,640]{2,1,0:T(8,128)(2,1)} all-to-all(bf16[16,64,640]{2,1,0:T(8,128)(2,1)} %bucket.1), channel_id=1, replica_groups=mesh['tm'=16,'head'=2] {'tm'}, dimensions={0} | all-to-all | bytes 2621440 | tf_op jit(solution)/shard_map/all_to_all | solution.py:442
  140.1 0.0 all-gather.15.cloned.1.call-update
  140.2 1.2 fusion.1
  141.4 0.7 select_reduce_fusion.sender_ref
  142.1 7.3 %all-gather.15.cloned.1.call-done = bf16[32,64,640]{2,1,0:T(8,128)(2,1)} async-done(((bf16[16,64,640]{2,1,0:T(8,128)(2,1)}), bf16[32,64,640]{2,1,0:T(8,128)(2,1)}) %all-gather.15.cloned.1.call-update) | async-done | bytes 2621456 | tf_op jit(solution)/shard_map/all_gather | solution.py:452
  149.4 19.1 %connect.1 = (bf16[768,2048]{1,0:T(8,128)(2,1)}, bf16[768,4096]{1,0:T(8,128)(2,1)}) custom-call(s32[12]{0:T(128)} %select_reduce_fusion.sender_ref, s32[1]{0:T(128)} %bitcast.my_ref, bf16[2,16,64,640]{3,2,1,0:T(8,128)(2,1)} %bitcast.51, bf16[2,1152,2048]{2,1,0:T(8,128)(2,1)} %bitcast.44, f32[1,4096]{1,0:T(1,128)} %bitcast.63), custom_call_target="tpu_custom_call" | custom-call | tf_op jit(solution)/shard_map/connect/pallas_call | solution.py:193
  168.5 4.8 %broadcast_multiply_fusion.1 = (f32[768,32]{0,1:T(8,128)S(1)}, f32[768,32]{0,1:T(8,128)S(1)}) fusion(f32[32]{0:T(128)S(1)} %exponential_negate_fusion, f32[32]{0:T(128)S(1)} %copy-done.7, bf16[768,4096]{1,0:T(8,128)(2,1)} %get-tuple-element.11, bf16[4096,32]{0,1:T(8,128)(2,1)S(1)} %copy-done), kind=kOutput, calls=%fused_computation.11 | convolution fusion | flops 201523200 | bytes 6750464 | tf_op jit(solution)/shard_map/dot_general | solution.py:460
  173.3 0.2 copy.55
  173.5 0.4 reduce_window_sum.22
  173.9 0.1 fusion.4
  174.0 0.1 copy.56
  174.2 0.1 broadcast_in_dim.66
  174.2 0.1 multiply_bitcast_fusion
  174.3 0.0 slice-start
  174.4 1.7 copy.51
  176.0 21.8 %convolution_convert_fusion.inner_ref = bf16[768,2048]{1,0:T(8,128)(2,1)} fusion(bf16[768,4096]{1,0:T(8,128)(2,1)} %get-tuple-element.11, bf16[4096,2048]{1,0:T(8,128)(2,1)} %param.24), kind=kOutput, calls=%fused_computation | convolution fusion | flops 12886474752 | bytes 26214400 | tf_op jit(solution)/shard_map/dot_general | solution.py:462
  197.9 0.0 slice-done
  197.9 4.3 %convolution_convert_fusion.2.write_ref = bf16[768,512]{1,0:T(8,128)(2,1)} fusion(bf16[768,4096]{1,0:T(8,128)(2,1)S(1)} %bitcast.46, bf16[4096,512]{1,0:T(8,128)(2,1)S(1)} %copy-done.10), kind=kOutput, calls=%fused_computation.2 | convolution fusion | flops 3221618688 | bytes 11272192 | tf_op jit(solution)/shard_map/dot_general | solution.py:463
  202.2 0.1 broadcast_in_dim.67
  202.3 0.1 broadcast_in_dim.68
  202.4 0.0 copy-start.8
  202.4 7.1 %final_state.1 = bf16[2048,128]{1,0:T(8,128)(2,1)} custom-call(bf16[768,2048]{1,0:T(8,128)(2,1)} %convolution_convert_fusion.inner_ref, bf16[768,512]{1,0:T(8,128)(2,1)} %convolution_convert_fusion.2.write_ref, f32[4,768,8]{2,1,0:T(8,128)} %bitcast.47), custom_call_target="tpu_custom_call" | custom-call | tf_op jit(solution)/shard_map/final_state/pallas_call | solution.py:243
  209.6 1.9 pad_maximum_fusion
  211.5 6.8 %all-to-all-start.3 = ((bf16[16,144,128]{2,1,0:T(8,128)(2,1)}), bf16[16,144,128]{2,1,0:T(8,128)(2,1)S(1)}, u32[]{:S(2)}, u32[]{:S(2)}) async-start(bf16[16,144,128]{2,1,0:T(8,128)(2,1)} %pad_maximum_fusion), calls=%async_computation.3 | async-start | bytes 1179648 | tf_op jit(solution)/shard_map/all_to_all | solution.py:348
  218.3 0.1 broadcast_in_dim.65
  218.4 0.7 reshape_reshape.4.skip_ref
  219.0 0.2 copy.47
  219.3 1.6 copy.48
  220.9 1.7 copy.49
  222.6 0.2 copy.53
  222.8 1.7 copy.54
  224.5 8.3 %convolution_convert_fusion.1.read_ref = bf16[768,512]{1,0:T(8,128)(2,1)} fusion(bf16[768,4096]{1,0:T(8,128)(2,1)} %get-tuple-element.11, bf16[4096,512]{1,0:T(8,128)(2,1)} %param.26), kind=kOutput, calls=%fused_computation.1 | convolution fusion | flops 3221618688 | bytes 11272192 | tf_op jit(solution)/shard_map/dot_general | solution.py:464
  232.7 2.2 all-to-all-done.3.arrived_ref
  234.9 0.1 reshape.116
  235.0 1.3 copy.52.decay_ref
  236.4 2.6 prefix.1
  239.0 4.7 %all-to-all-start.4 = ((bf16[16,128,128]{2,1,0:T(8,128)(2,1)}), bf16[16,128,128]{2,1,0:T(8,128)(2,1)S(1)}, u32[]{:S(2)}, u32[]{:S(2)}) async-start(bf16[16,128,128]{2,1,0:T(8,128)(2,1)} %prefix.1), calls=%async_computation.4 | async-start | bytes 1048576 | tf_op jit(solution)/shard_map/all_to_all | solution.py:358
  243.7 24.6 %local_outputs.1.local_ref = f32[768,2048]{1,0:T(8,128)} custom-call(bf16[768,2048]{1,0:T(8,128)(2,1)} %convolution_convert_fusion.inner_ref, bf16[768,512]{1,0:T(8,128)(2,1)} %convolution_convert_fusion.2.write_ref, bf16[768,512]{1,0:T(8,128)(2,1)} %convolution_convert_fusion.1.read_ref, f32[4,768,8]{2,1,0:T(8,128)} %bitcast.54, f32[4,8,768]{2,1,0:T(8,128)} %bitcast.59, ...), custom_call_target="tpu_custom_call" | custom-call | flops 20000000000 | bytes 20000000 | tf_op jit(solution)/shard_map/local_outputs/pallas_call | solution.py:308
  268.3 0.0 all-to-all-done.4
  268.3 0.0 copy-start.1
  268.3 0.8 copy-done.3
  269.1 13.9 %finish.1 = bf16[768,2048]{1,0:T(8,128)(2,1)} custom-call(f32[768,2048]{1,0:T(8,128)} %local_outputs.1.local_ref, bf16[768,512]{1,0:T(8,128)(2,1)} %convolution_convert_fusion.1.read_ref, bf16[2048,128]{1,0:T(8,128)(2,1)} %bitcast.53, f32[4,768,8]{2,1,0:T(8,128)} %bitcast.48, f32[1,2048]{1,0:T(1,128)} %bitcast.65), custom_call_target="tpu_custom_call" | custom-call | tf_op jit(solution)/shard_map/finish/pallas_call | solution.py:384
  (42 shorter events, 0.2 us)
Async XLA Ops:
  7.2 161.4 %copy-start = (bf16[4096,32]{0,1:T(8,128)(2,1)S(1)}, bf16[4096,32]{0,1:T(8,128)(2,1)}, u32[]{:S(2)}) copy-start(bf16[4096,32]{0,1:T(8,128)(2,1)} %param.27) | copy-start | bytes 786436
  7.2 15.8 %all-gather.9.cloned.1.call-start = ((), (), s32[]{:S(2)}) async-start(), calls=%async_computation.5 | async-start | bytes 2654208 | tf_op jit(solution)/shard_map/all_gather | solution.py:425
  9.4 34.9 %all-gather.11.cloned.1.call-start = ((), (), s32[]{:S(2)}) async-start(), calls=%async_computation.6 | async-start | bytes 7962624 | tf_op jit(solution)/shard_map/all_gather | solution.py:425
  12.9 0.8 copy-start.11
  12.9 1.4 copy-start.6
  12.9 2.7 copy-start.12
  12.9 83.8 %all-gather.13.cloned.1.call-start = ((), (), s32[]{:S(2)}) async-start(), calls=%async_computation.7 | async-start | bytes 14155776 | tf_op jit(solution)/shard_map/all_gather | solution.py:426
  13.7 9.3 %copy-start.9 = (s32[12]{0:T(128)}, s32[12]{0:T(128)S(1)}, u32[]{:S(2)}) copy-start(s32[12]{0:T(128)S(1)} %broadcast_multiply_fusion.2) | copy-start | bytes 148
  40.7 48.5 %all-to-all-start = ((bf16[2,3,64,576]{3,2,1,0:T(8,128)(2,1)}), bf16[2,3,64,576]{3,2,1,0:T(8,128)(2,1)S(1)}, u32[]{:S(2)}, u32[]{:S(2)}) async-start(bf16[2,3,64,576]{3,2,1,0:T(8,128)(2,1)} %attend.2), calls=%async_computation | async-start | bytes 983040 | tf_op jit(solution)/shard_map/all_to_all | solution.py:431
  44.2 105.2 %all-gather.15.cloned.1.call-start = ((), (), s32[]{:S(2)}) async-start(), calls=%async_computation.8 | async-start | bytes 3932160 | tf_op jit(solution)/shard_map/all_gather | solution.py:452
  89.2 7.6 %copy-start.4 = (bf16[2,3,64,576]{3,2,1,0:T(8,128)(2,1)}, bf16[2,3,64,576]{3,2,1,0:T(8,128)(2,1)S(1)}, u32[]{:S(2)}) copy-start(bf16[2,3,64,576]{3,2,1,0:T(8,128)(2,1)S(1)} %all-to-all-done.refs_0_) | copy-start | bytes 1327108
  96.8 43.4 %copy-start.13 = (f32[32]{0:T(128)S(1)}, f32[32]{0:T(128)}, u32[]{:S(2)}) copy-start(f32[32]{0:T(128)} %param.29) | copy-start | bytes 388
  149.4 19.1 %copy-start.7 = (f32[32]{0:T(128)S(1)}, f32[32]{0:T(128)}, u32[]{:S(2)}) copy-start(f32[32]{0:T(128)} %param.28) | copy-start | bytes 388
  174.3 23.5 %slice-start = ((s8[6291456]{0:T(1024)(128)(4,1)}), s8[2097152]{0:T(1024)(128)(4,1)S(1)}, s32[]{:S(2)}) async-start(s8[6291456]{0:T(1024)(128)(4,1)} %bitcast.45), calls=%async_computation.9 | async-start | bytes 4194304
  176.0 21.9 %slice-start.1 = ((s8[6291456]{0:T(1024)(128)(4,1)}), s8[4194304]{0:T(1024)(128)(4,1)S(1)}, s32[]{:S(2)}) async-start(s8[6291456]{0:T(1024)(128)(4,1)} %bitcast.45), calls=%async_computation.10 | async-start | bytes 8388608
  176.0 21.9 %copy-start.10 = (bf16[4096,512]{1,0:T(8,128)(2,1)S(1)}, bf16[4096,512]{1,0:T(8,128)(2,1)}, u32[]{:S(2)}) copy-start(bf16[4096,512]{1,0:T(8,128)(2,1)} %param.25) | copy-start | bytes 12582916
  202.4 15.9 %copy-start.8 = (f32[32]{0:T(128)S(1)}, f32[32]{0:T(128)}, u32[]{:S(2)}) copy-start(f32[32]{0:T(128)} %param.30) | copy-start | bytes 388
  211.5 23.4 %all-to-all-start.3 = ((bf16[16,144,128]{2,1,0:T(8,128)(2,1)}), bf16[16,144,128]{2,1,0:T(8,128)(2,1)S(1)}, u32[]{:S(2)}, u32[]{:S(2)}) async-start(bf16[16,144,128]{2,1,0:T(8,128)(2,1)} %pad_maximum_fusion), calls=%async_computation.3 | async-start | bytes 1179648 | tf_op jit(solution)/shard_map/all_to_all | solution.py:348
  219.3 13.5 %copy-start.5 = (f32[768,4,8]{0,2,1:T(8,128)}, f32[768,4,8]{0,2,1:T(8,128)S(1)}, u32[]{:S(2)}) copy-start(f32[768,4,8]{0,2,1:T(8,128)S(1)} %mul.29) | copy-start | bytes 294916
  234.9 1.5 copy-start.2
  239.0 29.4 %all-to-all-start.4 = ((bf16[16,128,128]{2,1,0:T(8,128)(2,1)}), bf16[16,128,128]{2,1,0:T(8,128)(2,1)S(1)}, u32[]{:S(2)}, u32[]{:S(2)}) async-start(bf16[16,128,128]{2,1,0:T(8,128)(2,1)} %prefix.1), calls=%async_computation.4 | async-start | bytes 1048576 | tf_op jit(solution)/shard_map/all_to_all | solution.py:358
  268.3 0.8 copy-start.3
  268.3 14.6 %copy-start.1 = (bf16[4096,32]{0,1:T(8,128)(2,1)S(1)}, bf16[4096,32]{0,1:T(8,128)(2,1)}, u32[]{:S(2)}) copy-start(bf16[4096,32]{0,1:T(8,128)(2,1)} %param.27) | copy-start | bytes 786436
Sparse Core Ops, SparseCore 0:
  10.1 12.8 all-gather.8
  25.1 16.4 all-gather.10
  43.2 22.8 all-gather.12
  140.2 9.1 all-gather.14
